TPU v7x, 512 devices: a whole 4x8x8 slice. The times are simulated.
512 devices in a mesh: gz: 8 (over z), pr: 16 (over y, core), pc: 4 (over x).
Axes of the slice: x: 4, y: 8, z: 8, core: 2. Of those that a mesh axis runs over, the one named last changes fastest.
Arguments:
- sep_rhs: bfloat16 [16, 3, 128, 128], P('pr'), may hold values from -6 to 6
- diag_inverse: bfloat16 [16, 3, 128, 128], P('pr'), may hold values from -0.5 to 0.5
- off_blocks: bfloat16 [16, 3, 12, 4, 128, 128], P('pr', None, None, 'pc'), may hold values from -0.109375 to 0.109375
- pattern: int32 [48, 48], replicated, may hold values 0 or 1
- sub_solution: bfloat16 [8, 16, 4, 1024, 128], P('gz', 'pr', 'pc'), may hold values from -6 to 6
- couple_low: bfloat16 [8, 16, 4, 384, 1024], P('gz', 'pr', 'pc'), may hold values from -0.03125 to 0.03125
- couple_up: bfloat16 [8, 16, 4, 1024, 384], P('gz', 'pr', 'pc'), may hold values from -0.3125 to 0.3125
Outputs:
- sep_solution: bfloat16 [16, 3, 128, 128], P('pr')
- sub_result: bfloat16 [8, 16, 4, 1024, 128], P('gz', 'pr', 'pc')
Inputs may be any that keep to these rules, and one draw needn't show every extreme that they name: `pattern`: only entries [i, j] with i // 16 > j // 16 are read; 1 marks a nonzero block.
All inputs are finite; a program needn't handle non-finite values.
Results may differ from a plain program's by a relative error of at most 0.02.
Values may be sent and summed in bfloat16 or wider, within the bound.
A program may use at most 64 MiB of HBM per device.

v0:
```python
import jax
import jax.numpy as jnp
from jax import lax
from jax.sharding import PartitionSpec as P


def per_device(sep_rhs, diag_inverse, off_blocks, pattern, sub_solution, couple_low, couple_up):
    row_index = lax.axis_index("pr")
    col_index = lax.axis_index("pc")
    row_count = lax.axis_size("pr")
    col_count = lax.axis_size("pc")
    inverse = diag_inverse[0]
    blocks = off_blocks[0, :, :, 0]
    levels = inverse.shape[0]
    block_width = inverse.shape[1]
    col_blocks = blocks.shape[1]
    block_count = levels * row_count
    own_sub = sub_solution[0, 0, 0]
    partial_value = jnp.dot(couple_low[0, 0, 0], own_sub, preferred_element_type=jnp.float32)
    rhs_local = sep_rhs[0].astype(jnp.float32)
    rhs_cols = own_sub.shape[1]
    summed = lax.psum(partial_value.astype(jnp.bfloat16), ("gz", "pc")).astype(jnp.float32)
    fed_rhs = rhs_local - summed.reshape(rhs_local.shape)
    rows_pattern = lax.dynamic_index_in_dim(
        pattern.reshape(levels, row_count, block_count), row_index, 1, keepdims=False
    )
    marks_forward = lax.dynamic_index_in_dim(
        rows_pattern.reshape(levels, col_blocks, col_count), col_index, 2, keepdims=False
    )
    cols_pattern = lax.dynamic_index_in_dim(
        jnp.transpose(pattern).reshape(levels, row_count, block_count), row_index, 1, keepdims=False
    )
    marks_backward = lax.dynamic_index_in_dim(
        cols_pattern.reshape(levels, col_blocks, col_count), col_index, 2, keepdims=False
    )
    col_levels = (jnp.arange(col_blocks, dtype=jnp.int32) * col_count + col_index) // row_count
    empty_cols = jnp.zeros((col_blocks, block_width, rhs_cols), jnp.bfloat16)

    def own_columns(level_blocks):
        flat = level_blocks.reshape(col_blocks, col_count, block_width, rhs_cols)
        return lax.dynamic_index_in_dim(flat, col_index, 1, keepdims=False)

    y_levels = jnp.zeros((levels, row_count, block_width, rhs_cols), jnp.bfloat16)
    for level in range(levels):
        if level == 0:
            residual = fed_rhs[level].astype(jnp.bfloat16)
        else:
            keep = (marks_forward[level] == 1) & (col_levels < level)
            masked = jnp.where(keep[:, None, None], own_columns(y_levels), empty_cols)
            part = jnp.einsum(
                "bst,btc->sc", blocks[level], masked, preferred_element_type=jnp.float32
            )
            total = lax.psum(part.astype(jnp.bfloat16), "pc").astype(jnp.float32)
            residual = (fed_rhs[level] - total).astype(jnp.bfloat16)
        solved = jnp.dot(inverse[level], residual, preferred_element_type=jnp.float32).astype(
            jnp.bfloat16
        )
        level_rows = lax.all_gather(solved[None], "pr", axis=0, tiled=True)
        y_levels = y_levels.at[level].set(level_rows)
    y_own = lax.dynamic_index_in_dim(y_levels, row_index, 1, keepdims=False)
    x_levels = jnp.zeros((levels, row_count, block_width, rhs_cols), jnp.bfloat16)
    for level in range(levels - 1, -1, -1):
        if level == levels - 1:
            x_levels = x_levels.at[level].set(y_levels[level])
        else:
            keep = (marks_backward[level] == 1) & (col_levels > level)
            masked = jnp.where(keep[:, None, None], own_columns(x_levels), empty_cols)
            part = jnp.einsum(
                "bst,btc->sc", blocks[level], masked, preferred_element_type=jnp.float32
            )
            total = lax.psum(part.astype(jnp.bfloat16), "pc").astype(jnp.float32)
            solved = (y_own[level].astype(jnp.float32) - total).astype(jnp.bfloat16)
            level_rows = lax.all_gather(solved[None], "pr", axis=0, tiled=True)
            x_levels = x_levels.at[level].set(level_rows)
    own_solution = lax.dynamic_index_in_dim(x_levels, row_index, 1, keepdims=False)
    full_cols = own_solution.shape[2]
    removed = jnp.dot(
        couple_up[0, 0, 0],
        own_solution.reshape(levels * block_width, full_cols),
        preferred_element_type=jnp.float32,
    )
    sub_result = (own_sub.astype(jnp.float32) - removed).astype(jnp.bfloat16)
    return (own_solution[None], sub_result[None, None, None])


def solution(mesh):
    return jax.shard_map(
        per_device,
        mesh=mesh,
        in_specs=(
            P("pr", None, None, None),
            P("pr", None, None, None),
            P("pr", None, None, "pc", None, None),
            P(),
            P("gz", "pr", "pc", None, None),
            P("gz", "pr", "pc", None, None),
            P("gz", "pr", "pc", None, None),
        ),
        out_specs=(P("pr", None, None, None), P("gz", "pr", "pc", None, None)),
        check_vma=False,
    )
```

profile of v0, /device:TPU:1, one launch (start us, length us, event | category | flops | bytes accessed | tf_op | source)
XLA Modules:
  0.0 342.4 jit_solution(462359540786047453)
XLA Ops:
  7.2 0.0 all-reduce.4.cloned.1.call-start
  7.3 1.6 convolution_convert_fusion
  8.9 0.8 copy.37
  9.7 0.8 copy.49
  10.5 0.1 reshape.352
  10.6 0.7 constant_dynamic-slice_fusion.4
  11.3 0.1 reshape.346
  11.4 0.2 fusion.51
  11.7 0.9 copy.36
  12.6 0.1 copy.35
  12.7 155.2 %all-reduce.4.cloned.1.call-done = bf16[3,128,128]{1,2,0:T(8,128)(2,1)} async-done(((bf16[3,128,128]{1,2,0:T(8,128)(2,1)}), bf16[3,128,128]{1,2,0:T(8,128)(2,1)}) %all-reduce.4.cloned.1.call-update) | async-done | bytes 98320 | tf_op jit(solution)/shard_map/psum | solution.py:22
  167.9 0.9 convert_subtract_fusion
  168.8 0.1 fusion.7
  168.9 23.2 %all-gather = bf16[2048,128]{0,1:T(8,128)(2,1)S(1)} all-gather(bf16[128,128]{0,1:T(8,128)(2,1)S(1)} %fusion.7), channel_id=2, replica_groups=mesh['gz'=8,'pr'=16,'pc'=4] {'pr'}, dimensions={0}, use_global_device_ids=true | all-gather | bytes 557056 | tf_op jit(solution)/shard_map/all_gather | solution.py:58
  192.1 0.1 copy.65
  192.3 0.1 copy.39
  192.4 0.3 scatter.20
  192.8 0.2 copy.63
  193.0 1.4 fusion.13
  194.4 11.9 %psum.36 = bf16[128,128]{0,1:T(8,128)(2,1)S(1)} all-reduce(bf16[128,128]{0,1:T(8,128)(2,1)S(1)} %fusion.13), channel_id=1, replica_groups=mesh['gz'=8,'pr'=16,'pc'=4] {'pc'}, use_global_device_ids=true, to_apply=%region_1.2 | all-reduce | flops 16384 | bytes 65536 | tf_op jit(solution)/shard_map/psum | solution.py:53
  206.3 0.1 fusion.8
  206.4 20.4 %all-gather.1 = bf16[2048,128]{0,1:T(8,128)(2,1)S(1)} all-gather(bf16[128,128]{0,1:T(8,128)(2,1)S(1)} %fusion.8), channel_id=3, replica_groups=mesh['gz'=8,'pr'=16,'pc'=4] {'pr'}, dimensions={0}, use_global_device_ids=true | all-gather | bytes 557056 | tf_op jit(solution)/shard_map/all_gather | solution.py:58
  226.8 0.1 copy.66
  226.9 0.2 copy_dynamic-update-slice_fusion.1
  227.2 0.2 copy.64
  227.4 1.4 fusion.12
  228.8 11.3 %psum.37 = bf16[128,128]{0,1:T(8,128)(2,1)S(1)} all-reduce(bf16[128,128]{0,1:T(8,128)(2,1)S(1)} %fusion.12), channel_id=1, replica_groups=mesh['gz'=8,'pr'=16,'pc'=4] {'pc'}, use_global_device_ids=true, to_apply=%region_2.3 | all-reduce | flops 16384 | bytes 65536 | tf_op jit(solution)/shard_map/psum | solution.py:53
  240.1 0.1 fusion.9
  240.2 20.2 %all-gather.2 = bf16[2048,128]{0,1:T(8,128)(2,1)S(1)} all-gather(bf16[128,128]{0,1:T(8,128)(2,1)S(1)} %fusion.9), channel_id=4, replica_groups=mesh['gz'=8,'pr'=16,'pc'=4] {'pr'}, dimensions={0}, use_global_device_ids=true | all-gather | bytes 557056 | tf_op jit(solution)/shard_map/all_gather | solution.py:58
  260.5 0.1 copy.67
  260.6 0.2 copy_dynamic-update-slice_fusion
  260.8 0.5 copy.47
  261.2 0.3 scatter.24
  261.5 1.1 copy-done.1
  262.7 1.4 fusion.11
  264.1 11.9 %psum.38 = bf16[128,128]{0,1:T(8,128)(2,1)S(1)} all-reduce(bf16[128,128]{0,1:T(8,128)(2,1)S(1)} %fusion.11), channel_id=1, replica_groups=mesh['gz'=8,'pr'=16,'pc'=4] {'pc'}, use_global_device_ids=true, to_apply=%region_3.4 | all-reduce | flops 16384 | bytes 65536 | tf_op jit(solution)/shard_map/psum | solution.py:71
  276.0 20.4 %all-gather.3 = bf16[2048,128]{0,1:T(8,128)(2,1)S(1)} all-gather(bf16[128,128]{0,1:T(8,128)(2,1)S(1)} %fusion.40), channel_id=5, replica_groups=mesh['gz'=8,'pr'=16,'pc'=4] {'pr'}, dimensions={0}, use_global_device_ids=true | all-gather | bytes 557056 | tf_op jit(solution)/shard_map/all_gather | solution.py:73
  296.4 0.3 copy.60
  296.7 0.9 constant_dynamic-update-slice_fusion.1
  297.5 1.5 fusion.10
  299.0 11.3 %psum.39 = bf16[128,128]{0,1:T(8,128)(2,1)S(1)} all-reduce(bf16[128,128]{0,1:T(8,128)(2,1)S(1)} %fusion.10), channel_id=1, replica_groups=mesh['gz'=8,'pr'=16,'pc'=4] {'pc'}, use_global_device_ids=true, to_apply=%region_4.5 | all-reduce | flops 16384 | bytes 65536 | tf_op jit(solution)/shard_map/psum | solution.py:71
  310.4 20.4 %all-gather.4 = bf16[2048,128]{0,1:T(8,128)(2,1)S(1)} all-gather(bf16[128,128]{0,1:T(8,128)(2,1)S(1)} %fusion.39), channel_id=6, replica_groups=mesh['gz'=8,'pr'=16,'pc'=4] {'pr'}, dimensions={0}, use_global_device_ids=true | all-gather | bytes 557056 | tf_op jit(solution)/shard_map/all_gather | solution.py:73
  330.7 0.3 copy.61
  331.0 0.8 constant_dynamic-update-slice_fusion
  331.8 0.9 constant_dynamic-slice_fusion
  332.7 1.5 fusion.63
  334.3 0.4 fusion.2
  334.7 0.8 copy.55
  (22 shorter events, 0.3 us)
Async XLA Ops:
  7.2 327.1 %copy-start = (bf16[1,1,1,1024,384]{4,3,2,1,0:T(8,128)(2,1)S(1)}, bf16[1,1,1,1024,384]{4,3,2,1,0:T(8,128)(2,1)}, u32[]{:S(2)}) copy-start(bf16[1,1,1,1024,384]{4,3,2,1,0:T(8,128)(2,1)} %param.25) | copy-start | bytes 2359300
  7.2 4.6 %copy-start.2 = (bf16[1,1,1,1024,128]{4,3,2,1,0:T(8,128)(2,1)S(1)}, bf16[1,1,1,1024,128]{4,3,2,1,0:T(8,128)(2,1)}, u32[]{:S(2)}) copy-start(bf16[1,1,1,1024,128]{4,3,2,1,0:T(8,128)(2,1)} %param.23) | copy-start | bytes 786436
  7.2 5.4 %copy-start.4 = (bf16[1,3,128,128]{3,2,1,0:T(8,128)(2,1)S(1)}, bf16[1,3,128,128]{3,2,1,0:T(8,128)(2,1)}, u32[]{:S(2)}) copy-start(bf16[1,3,128,128]{3,2,1,0:T(8,128)(2,1)} %param.19) | copy-start | bytes 294916
  7.2 161.6 %copy-start.5 = (bf16[1,3,128,128]{3,2,1,0:T(8,128)(2,1)S(1)}, bf16[1,3,128,128]{3,2,1,0:T(8,128)(2,1)}, u32[]{:S(2)}) copy-start(bf16[1,3,128,128]{3,2,1,0:T(8,128)(2,1)} %param.20) | copy-start | bytes 294916
  7.2 160.7 %all-reduce.4.cloned.1.call-start = ((), (), s32[]{:S(2)}) async-start(), calls=%async_computation | async-start | bytes 196608 | tf_op jit(solution)/shard_map/psum | solution.py:22
  261.5 1.2 copy-start.1
  310.3 23.9 %copy-start.3 = (bf16[1,1,1,1024,128]{3,4,2,1,0:T(8,128)(2,1)S(1)}, bf16[1,1,1,1024,128]{3,4,2,1,0:T(8,128)(2,1)}, u32[]{:S(2)}) copy-start(bf16[1,1,1,1024,128]{3,4,2,1,0:T(8,128)(2,1)} %copy.36) | copy-start | bytes 786436
Sparse Core Ops, SparseCore 0:
  12.0 155.8 all-reduce.3
where the time goes:
time: 343 us; the launch traced here: 342 us
  waiting for transfers between devices  155 us (45%)
  blocking collectives  151 us (44%)
  between operations  14.3 us (4%)
  local copies, waits for them, and re-layouts  12.5 us (4%)
  matrix products  8.08 us (2%)
    psum x1, waiting for transfers between devices, per_device(): lax.psum(partial_value.astype(jnp.bfloat16), ('gz', 'pc'))  155 us
    all_gather x5, blocking collectives, per_device(): level_rows = lax.all_gather(solved[None], 'pr', axis=0, tiled=True)  105 us
    psum x4, blocking collectives, per_device(): total = lax.psum(part.astype(jnp.bfloat16), 'pc').astype(jnp.float32)  46.4 us
  transfers between devices with their start and end apart: 1, of which 1 were waited for; matrix products, arithmetic and copies ran while one was open for 1% of the time, Pallas kernels for 0%

commit v1 on v0

v1 whole, which is shorter than its diff:
```python
import functools

import jax
import jax.numpy as jnp
from jax import lax
from jax.experimental import pallas as pl
from jax.experimental.pallas import tpu as pltpu
from jax.sharding import PartitionSpec as P

F32 = jnp.float32
BF16 = jnp.bfloat16
MESH = pl.DeviceIdType.MESH


def nt(a, b):
    return lax.dot_general(a, b, (((1,), (1,)), ((), ())), preferred_element_type=F32)


def ring_order(n):
    return sorted(range(1, n), key=lambda r: (-min(r, n - r), r))


def kernel(
    dims,
    rhs_hbm, inv_hbm, blk_hbm, pat_hbm, sub_hbm, low_hbm, up_hbm,
    x_hbm, res_hbm,
    sub_v, low_v, up_v, inv_v, rhs_v, blk_v, pat_s,
    w_v, rhs_t, zsend, zrecv, fsend, frecv, psend, precv, ysend, yrecv, xz, acc, res_v, x_v,
    in_sem, zs_sem, zr_sem, fs_sem, fr_sem, ps_sem, pr_sem, ys_sem, yr_sem, xs_sem, xr_sem, out_sem,
):
    n_g, n_p, n_q, levels, width, n_b = dims
    g = lax.axis_index("gz")
    p = lax.axis_index("pr")
    q = lax.axis_index("pc")
    nb = n_p // n_q
    own = lax.rem(p, n_q) == q
    own_b = p // n_q

    loads = [
        pltpu.make_async_copy(sub_hbm, sub_v, in_sem.at[0]),
        pltpu.make_async_copy(low_hbm.at[pl.ds(0, width)], low_v.at[pl.ds(0, width)], in_sem.at[1]),
        pltpu.make_async_copy(
            low_hbm.at[pl.ds(width, (levels - 1) * width)],
            low_v.at[pl.ds(width, (levels - 1) * width)],
            in_sem.at[2],
        ),
        pltpu.make_async_copy(rhs_hbm, rhs_v, in_sem.at[3]),
        pltpu.make_async_copy(inv_hbm, inv_v, in_sem.at[4]),
        pltpu.make_async_copy(pat_hbm, pat_s, in_sem.at[5]),
        pltpu.make_async_copy(blk_hbm, blk_v, in_sem.at[6]),
        pltpu.make_async_copy(up_hbm, up_v, in_sem.at[7]),
    ]
    for c in loads:
        c.start()

    def z_peer(r):
        return {"gz": lax.rem(g + r, n_g)}

    def x_peer(r):
        return {"pc": lax.rem(q + r, n_q)}

    def y_peer(r):
        return {"pr": lax.rem(p + r, n_p)}

    barrier = pltpu.get_barrier_semaphore()
    for r in ring_order(n_g):
        pl.semaphore_signal(barrier, inc=1, device_id=z_peer(r), device_id_type=MESH)
    for r in ring_order(n_p):
        pl.semaphore_signal(barrier, inc=1, device_id=y_peer(r), device_id_type=MESH)
    for r in ring_order(n_q):
        pl.semaphore_signal(barrier, inc=1, device_id=x_peer(r), device_id_type=MESH)

    def remote(src, dst, ssem, rsem, peer):
        return pltpu.make_async_remote_copy(
            src_ref=src, dst_ref=dst, send_sem=ssem, recv_sem=rsem, device_id=peer, device_id_type=MESH
        )

    sends = []

    def partial_update(a):
        part = jnp.dot(low_v[a * width : (a + 1) * width, :], sub_v[...], preferred_element_type=F32)
        flipped = jnp.transpose(part).astype(BF16)
        zsend[a] = flipped.reshape(n_g, flipped.shape[0] // n_g, width)

    def z_copy(a, r):
        return remote(
            zsend.at[a, lax.rem(g + r, n_g)], zrecv.at[a, r - 1], zs_sem.at[a, r - 1], zr_sem.at[a, r - 1], z_peer(r)
        )

    loads[0].wait()
    loads[1].wait()
    partial_update(0)
    pl.semaphore_wait(barrier, n_g + n_p + n_q - 3)
    for r in ring_order(n_g):
        c = z_copy(0, r)
        c.start()
        sends.append(c)
    loads[2].wait()
    for a in range(1, levels):
        partial_update(a)
        for r in ring_order(n_g):
            c = z_copy(a, r)
            c.start()
            sends.append(c)

    loads[3].wait()
    for a in range(levels):
        rhs_t[a] = jnp.transpose(rhs_v[a].astype(F32)).reshape(n_g, rhs_t.shape[2], width)
    loads[4].wait()
    loads[5].wait()
    loads[6].wait()

    def masked_blocks(row_level, col_level):
        slot = row_level * (levels - 1) + (col_level if col_level < row_level else col_level - 1)
        for b in range(nb):
            i = row_level * n_p + p
            j = col_level * n_p + b * n_q + q
            mark = pat_s[i, j] if col_level < row_level else pat_s[j, i]
            block = blk_v[row_level, col_level * nb + b]
            w_v[slot, :, b * width : (b + 1) * width] = jnp.where(mark == 1, block, jnp.zeros_like(block))

    def weights(row_level, col_level):
        slot = row_level * (levels - 1) + (col_level if col_level < row_level else col_level - 1)
        return w_v[slot]

    for col in range(levels):
        for row in range(col + 1, levels):
            masked_blocks(row, col)

    def z_total(a):
        for r in range(1, n_g):
            z_copy(a, r).wait_recv()
        total = zsend[a, g].astype(F32)
        for r in range(1, n_g):
            total = total + zrecv[a, r - 1].astype(F32)
        return total.astype(BF16)

    def exchange(value, src, dst, ssem, rsem):
        src[...] = value
        copies = []
        for r in ring_order(n_q):
            c = remote(src, dst.at[r - 1], ssem.at[r - 1], rsem.at[r - 1], x_peer(r))
            c.start()
            copies.append(c)
            sends.append(c)
        return copies

    def collected(value, copies, dst):
        for c in copies:
            c.wait_recv()
        half = n_q // 2
        total = None
        for k in range(half):
            first = value.astype(F32) if k == 0 else dst[k - 1].astype(F32)
            pair = first + dst[k + half - 1].astype(F32)
            total = pair if total is None else total + pair
        return total

    def f_exchange(a):
        value = z_total(a)
        return value, exchange(value, fsend.at[a], frecv.at[a], fs_sem.at[a], fr_sem.at[a])

    def fed(a, started):
        value, copies = started
        return rhs_t[a, g] - collected(value, copies, frecv.at[a])

    def y_copy(k, r):
        return remote(ysend.at[k], yrecv.at[k, own_b], ys_sem.at[k, r - 1], yr_sem.at[k, own_b], y_peer(r))

    def broadcast(k, value):
        ysend[k] = value

        @pl.when(own)
        def _():
            for r in ring_order(n_p):
                y_copy(k, r).start()
            yrecv[k, own_b] = value

    def gathered(k):
        for b in range(nb):

            @pl.when(b * n_q + q != p)
            def _(b=b):
                remote(ysend.at[k], yrecv.at[k, b], ys_sem.at[k, 0], yr_sem.at[k, b], y_peer(1)).wait_recv()

        return jnp.concatenate([yrecv[k, b] for b in range(nb)], axis=1)

    def spread(a, value):
        xz[a, g] = value
        for r in ring_order(n_g):
            c = remote(xz.at[a, g], xz.at[a, g], xs_sem.at[a, r - 1], xr_sem.at[a, r - 1], z_peer(r))
            c.start()
            sends.append(c)

    def solve(a, resid):
        return nt(resid.astype(BF16), inv_v[a]).astype(BF16)

    started = f_exchange(0)
    fed_a = fed(0, started)
    y = [solve(0, fed_a)]
    broadcast(0, y[0])
    later = [f_exchange(a) for a in range(1, levels)]
    for row in range(levels):
        for col in range(row + 1, levels):
            masked_blocks(row, col)
    feds = [None] + [fed(a, later[a - 1]) for a in range(1, levels)]

    pending = [None] * levels
    for a in range(1, levels):
        block = gathered(a - 1)
        part = nt(block, weights(a, a - 1))
        part = part if pending[a] is None else pending[a] + part
        value = part.astype(BF16)
        copies = exchange(value, psend.at[a - 1], precv.at[a - 1], ps_sem.at[a - 1], pr_sem.at[a - 1])
        for later_a in range(a + 1, levels):
            more = nt(block, weights(later_a, a - 1))
            pending[later_a] = more if pending[later_a] is None else pending[later_a] + more
        total = collected(value, copies, precv.at[a - 1])
        y.append(solve(a, feds[a] - total))
        broadcast(a, y[a])

    spread(levels - 1, y[levels - 1])
    pending = [None] * levels
    for a in range(levels - 2, -1, -1):
        k = 2 * (levels - 1) - 1 - a
        source = {levels - 2: levels - 1}.get(a, levels + (levels - 2 - (a + 1)))
        block = gathered(source)
        part = nt(block, weights(a, a + 1))
        part = part if pending[a] is None else pending[a] + part
        value = part.astype(BF16)
        copies = exchange(value, psend.at[k], precv.at[k], ps_sem.at[k], pr_sem.at[k])
        for later_a in range(a - 1, -1, -1):
            more = nt(block, weights(later_a, a + 1))
            pending[later_a] = more if pending[later_a] is None else pending[later_a] + more
        total = collected(value, copies, precv.at[k])
        x = (y[a].astype(F32) - total).astype(BF16)
        if a > 0:
            broadcast(levels + (levels - 2 - a), x)
        spread(a, x)

    loads[7].wait()
    rows = res_v.shape[0]
    n_c = 4
    chunk = rows // n_c
    stores = []
    for a in range(levels - 1, -1, -1):
        for r in range(1, n_g):
            remote(xz.at[a, g], xz.at[a, g], xs_sem.at[a, r - 1], xr_sem.at[a, r - 1], z_peer(r)).wait_recv()
        full = xz[a].reshape(n_g * xz.shape[2], width)
        for c in range(n_c):
            span = pl.ds(c * chunk, chunk)
            before = sub_v[span, :].astype(F32) if a == levels - 1 else acc[span, :]
            after = before - nt(up_v[span, a * width : (a + 1) * width], full)
            if a > 0:
                acc[span, :] = after
            else:
                res_v[span, :] = after.astype(BF16)
                store = pltpu.make_async_copy(res_v.at[span], res_hbm.at[span], out_sem.at[c])
                store.start()
                stores.append(store)
        x_v[a] = jnp.transpose(full.astype(F32)).astype(BF16)
    store = pltpu.make_async_copy(x_v, x_hbm, out_sem.at[n_c])
    store.start()
    stores.append(store)

    for c in sends:
        c.wait_send()

    @pl.when(own)
    def _():
        for k in range(2 * levels - 2):
            for r in range(1, n_p):
                y_copy(k, r).wait_send()

    for store in stores:
        store.wait()


def per_device(dims, sep_rhs, diag_inverse, off_blocks, pattern, sub_solution, couple_low, couple_up):
    n_g, n_p, n_q, levels, width, n_b = dims
    sub = sub_solution.reshape(sub_solution.shape[-2:])
    low = couple_low.reshape(couple_low.shape[-2:])
    up = couple_up.reshape(couple_up.shape[-2:])
    rhs = sep_rhs.reshape(sep_rhs.shape[1:])
    inv = diag_inverse.reshape(diag_inverse.shape[1:])
    blk = off_blocks.reshape(levels, n_b, width, width)
    rows, cols = sub.shape
    piece = cols // n_g
    nb = n_p // n_q
    n_bc = 2 * levels - 2
    dma = pltpu.SemaphoreType.DMA
    x, res = pl.pallas_call(
        functools.partial(kernel, dims),
        out_shape=(
            jax.ShapeDtypeStruct(rhs.shape, BF16),
            jax.ShapeDtypeStruct(sub.shape, BF16),
        ),
        in_specs=[pl.BlockSpec(memory_space=pl.ANY)] * 7,
        out_specs=(pl.BlockSpec(memory_space=pl.ANY),) * 2,
        scratch_shapes=[
            pltpu.VMEM(sub.shape, BF16),
            pltpu.VMEM(low.shape, BF16),
            pltpu.VMEM(up.shape, BF16),
            pltpu.VMEM(inv.shape, BF16),
            pltpu.VMEM(rhs.shape, BF16),
            pltpu.VMEM(blk.shape, BF16),
            pltpu.SMEM(pattern.shape, jnp.int32),
            pltpu.VMEM((levels * (levels - 1), width, nb * width), BF16),
            pltpu.VMEM((levels, n_g, piece, width), F32),
            pltpu.VMEM((levels, n_g, piece, width), BF16),
            pltpu.VMEM((levels, n_g - 1, piece, width), BF16),
            pltpu.VMEM((levels, piece, width), BF16),
            pltpu.VMEM((levels, n_q - 1, piece, width), BF16),
            pltpu.VMEM((n_bc, piece, width), BF16),
            pltpu.VMEM((n_bc, n_q - 1, piece, width), BF16),
            pltpu.VMEM((n_bc, piece, width), BF16),
            pltpu.VMEM((n_bc, nb, piece, width), BF16),
            pltpu.VMEM((levels, n_g, piece, width), BF16),
            pltpu.VMEM(sub.shape, F32),
            pltpu.VMEM(sub.shape, BF16),
            pltpu.VMEM(rhs.shape, BF16),
            dma((8,)),
            dma((levels, n_g - 1)),
            dma((levels, n_g - 1)),
            dma((levels, n_q - 1)),
            dma((levels, n_q - 1)),
            dma((n_bc, n_q - 1)),
            dma((n_bc, n_q - 1)),
            dma((n_bc, n_p - 1)),
            dma((n_bc, nb)),
            dma((levels, n_g - 1)),
            dma((levels, n_g - 1)),
            dma((5,)),
        ],
        compiler_params=pltpu.CompilerParams(collective_id=0, has_side_effects=True),
    )(rhs, inv, blk, pattern, sub, low, up)
    return x[None], res[None, None, None]


def solution(mesh):
    n_g, n_p, n_q = mesh.shape["gz"], mesh.shape["pr"], mesh.shape["pc"]

    def step(*args):
        levels, width = args[1].shape[1], args[1].shape[2]
        dims = (n_g, n_p, n_q, levels, width, args[2].shape[2])
        return per_device(dims, *args)

    return jax.shard_map(
        step,
        mesh=mesh,
        in_specs=(
            P("pr", None, None, None),
            P("pr", None, None, None),
            P("pr", None, None, "pc", None, None),
            P(),
            P("gz", "pr", "pc", None, None),
            P("gz", "pr", "pc", None, None),
            P("gz", "pr", "pc", None, None),
        ),
        out_specs=(P("pr", None, None, None), P("gz", "pr", "pc", None, None)),
        check_vma=False,
    )
```

time: 343 us -> 64.9 us (0.19)
  waiting for transfers between devices: 155 us -> 0 us
  blocking collectives: 151 us -> 0 us
  Pallas kernels: 0 us -> 60.3 us
  between operations: 14.3 us -> 0.64 us
  local copies, waits for them, and re-layouts: 12.5 us -> 3.21 us
  matrix products: 8.08 us -> 0 us
    psum x1 -> x0, waiting for transfers between devices: 155 us -> none  [per_device(): lax.psum(partial_value.astype(jnp.bfloat16), ('gz', 'pc'))]
    all_gather x5 -> x0, blocking collectives: 105 us -> none  [per_device(): level_rows = lax.all_gather(solved[None], 'pr', axis=0, tiled=True)]
    pallas_call x0 -> x1, Pallas kernels: none -> 60.3 us  [per_device(): pl.pallas_call(functools.partial(kernel, dims), out_shape=(jax.ShapeDtype...]
    psum x4 -> x0, blocking collectives: 46.4 us -> none  [per_device(): total = lax.psum(part.astype(jnp.bfloat16), 'pc').astype(jnp.float32)]
    dot_general x9 -> x0, matrix products: 8.08 us -> none  [the longest x4 5.66 us: per_device(): jnp.einsum('bst,btc->sc', blocks[level], masked, preferred_element_type=j...]
  transfers between devices with their start and end apart: 1 -> 0, of which waited for: 1 -> 0; matrix products, arithmetic and copies ran while one was open for 1% -> 0% of each run, Pallas kernels for 0% -> 0%
where the time goes in v1:
time: 64.9 us; the launch traced here: 64.2 us
  Pallas kernels  60.3 us (93%)
  local copies, waits for them, and re-layouts  3.21 us (5%)
    pallas_call x1, Pallas kernels, per_device(): pl.pallas_call(functools.partial(kernel, dims), out_shape=(jax.ShapeDtype...  60.3 us
    unnamed x2, local copies, waits for them, and re-layouts  3.21 us

profile of v1, /device:TPU:1, one launch (start us, length us, event | category | flops | bytes accessed | tf_op | source)
XLA Modules:
  0.0 64.2 jit_solution(11076275277672013863)
XLA Ops:
  0.6 60.3 %shard_map.86 = (bf16[3,128,128]{2,1,0:T(8,128)(2,1)}, bf16[1024,128]{1,0:T(8,128)(2,1)}) custom-call(bf16[3,128,128]{2,1,0:T(8,128)(2,1)} %bitcast.13, bf16[3,128,128]{2,1,0:T(8,128)(2,1)} %bitcast.14, bf16[3,12,128,128]{3,2,1,0:T(8,128)(2,1)} %bitcast.8, s32[48,48]{1,0:T(8,128)} %pat_hbm.1, bf16[1024,128]{1,0:T(8,128)(2,1)} %bitcast.11, ...), custom_call_target="tpu_custom_call" | custom-call | tf_op jit(solution)/shard_map/pallas_call | solution.py:292
  60.9 1.5 %copy.11 = bf16[1,3,128,128]{3,2,1,0:T(8,128)(2,1)} copy(bf16[1,3,128,128]{3,2,1,0:T(8,128)(2,1)} %bitcast.15) | data formatting | bytes 196608
  62.5 1.7 %copy.12 = bf16[1,1,1,1024,128]{4,3,2,1,0:T(8,128)(2,1)} copy(bf16[1,1,1,1024,128]{4,3,2,1,0:T(8,128)(2,1)} %bitcast.12) | data formatting | bytes 524288

commit v2 on v1

v2 whole, which is shorter than its diff:
```python
import functools

import jax
import jax.numpy as jnp
from jax import lax
from jax.experimental import pallas as pl
from jax.experimental.pallas import tpu as pltpu
from jax.sharding import PartitionSpec as P

F32 = jnp.float32
BF16 = jnp.bfloat16
MESH = pl.DeviceIdType.MESH


def nt(a, b):
    return lax.dot_general(a, b, (((1,), (1,)), ((), ())), preferred_element_type=F32)


def ring_order(n):
    return sorted(range(1, n), key=lambda r: (-min(r, n - r), r))


def kernel(
    dims,
    rhs_hbm, inv_hbm, blk_hbm, pat_hbm, sub_hbm, low_hbm, up_hbm,
    x_v, res_v,
    sub_v, low_v, up_v, inv_v, rhs_v, blk_v, pat_s,
    w_v, rhs_t, zsend, zrecv, fsend, frecv, psend, precv, bsend, brecv, ysend, yrecv, xz, acc, u_piece, u_all, f_all, prod,
    in_sem, zs_sem, zr_sem, fs_sem, fr_sem, ps_sem, pr_sem, ys_sem, yr_sem, xs_sem, xr_sem, us_sem, ur_sem, ws_sem, wr_sem, ds_sem, dr_sem,
):
    n_g, n_p, n_q, levels, width, n_b = dims
    g = lax.axis_index("gz")
    p = lax.axis_index("pr")
    q = lax.axis_index("pc")
    nb = n_p // n_q
    own = lax.rem(p, n_q) == q
    own_b = p // n_q

    part_rows = prod.shape[1]
    halves = width // part_rows

    rest = pl.ds(width, (levels - 1) * width)
    pairs = (
        (sub_hbm, sub_v),
        (low_hbm.at[pl.ds(0, width)], low_v.at[pl.ds(0, width)]),
        (low_hbm.at[rest], low_v.at[rest]),
        (blk_hbm, blk_v),
        (pat_hbm, pat_s),
        (rhs_hbm, rhs_v),
        (inv_hbm, inv_v),
        (up_hbm, up_v),
    )
    loads = [pltpu.make_async_copy(a, b, in_sem.at[k]) for k, (a, b) in enumerate(pairs)]
    for c in loads:
        c.start()

    def z_peer(r):
        return {"gz": lax.rem(g + r, n_g)}

    def x_peer(r):
        return {"pc": lax.rem(q + r, n_q)}

    def y_peer(r):
        return {"pr": lax.rem(p + r, n_p)}

    barrier = pltpu.get_barrier_semaphore()
    for r in ring_order(n_g):
        pl.semaphore_signal(barrier, inc=1, device_id=z_peer(r), device_id_type=MESH)
    for r in ring_order(n_p):
        pl.semaphore_signal(barrier, inc=1, device_id=y_peer(r), device_id_type=MESH)
    for r in ring_order(n_q):
        pl.semaphore_signal(barrier, inc=1, device_id=x_peer(r), device_id_type=MESH)

    def remote(src, dst, ssem, rsem, peer):
        return pltpu.make_async_remote_copy(
            src_ref=src, dst_ref=dst, send_sem=ssem, recv_sem=rsem, device_id=peer, device_id_type=MESH
        )

    sends = []

    def partial_update(a):
        part = jnp.dot(low_v[a * width : (a + 1) * width, :], sub_v[...], preferred_element_type=F32)
        flipped = jnp.transpose(part).astype(BF16)
        zsend[a] = flipped.reshape(n_g, flipped.shape[0] // n_g, width)

    def z_copy(a, r):
        return remote(
            zsend.at[a, lax.rem(g + r, n_g)], zrecv.at[a, r - 1], zs_sem.at[a, r - 1], zr_sem.at[a, r - 1], z_peer(r)
        )

    loads[0].wait()
    loads[1].wait()
    partial_update(0)
    pl.semaphore_wait(barrier, n_g + n_p + n_q - 3)
    for r in ring_order(n_g):
        c = z_copy(0, r)
        c.start()
        sends.append(c)
    loads[2].wait()
    for a in range(1, levels):
        partial_update(a)
        for r in ring_order(n_g):
            c = z_copy(a, r)
            c.start()
            sends.append(c)

    def slot_of(row_level, col_level):
        return row_level * (levels - 1) + (col_level if col_level < row_level else col_level - 1)

    def masked_blocks(row_level, col_level):
        for b in range(nb):
            i = row_level * n_p + p
            j = col_level * n_p + b * n_q + q
            mark = pat_s[i, j] if col_level < row_level else pat_s[j, i]
            block = blk_v[row_level, col_level * nb + b]
            w_v[slot_of(row_level, col_level), :, b * width : (b + 1) * width] = jnp.where(
                mark == 1, block, jnp.zeros_like(block)
            )

    def weights(row_level, col_level):
        return w_v[slot_of(row_level, col_level)]

    first, second = slot_of(0, 1), slot_of(1, 2)
    loads[3].wait()
    loads[4].wait()
    masked_blocks(0, 1)
    masked_blocks(1, 2)

    def f_copy(r):
        return remote(w_v.at[first], f_all.at[r - 1], ws_sem.at[r - 1], wr_sem.at[r - 1], x_peer(r))

    def u_copy(r):
        return remote(u_piece.at[g % halves], u_all.at[p], us_sem.at[r - 1], ur_sem.at[r - 1], y_peer(r))

    def d_copy(r):
        return remote(prod.at[g], prod.at[g], ds_sem.at[r - 1], dr_sem.at[r - 1], z_peer(r))

    for r in ring_order(n_q):
        c = f_copy(r)
        c.start()
        sends.append(c)
    mine = w_v[second, :, pl.ds(pl.multiple_of(g // halves * width, width), width)]
    u_piece[...] = jnp.transpose(mine.astype(F32)).astype(BF16).reshape(halves, part_rows, width)
    for r in ring_order(n_p):
        c = u_copy(r)
        c.start()
        sends.append(c)
    u_all[p] = u_piece[g % halves]

    loads[5].wait()
    for a in range(levels):
        rhs_t[a] = jnp.transpose(rhs_v[a].astype(F32)).reshape(n_g, rhs_t.shape[2], width)
    for row_level in range(1, levels):
        for col_level in range(row_level):
            masked_blocks(row_level, col_level)
    masked_blocks(0, 2)
    loads[6].wait()

    def form_product():
        for r in range(1, n_p):
            u_copy(r).wait_recv()
        total = None
        for r in range(n_q):
            if r:
                f_copy(r).wait_recv()
            left = weights(0, 1) if r == 0 else f_all[r - 1]
            from_q = lax.rem(q + n_q - r, n_q)
            right = jnp.concatenate([u_all[b * n_q + from_q] for b in range(nb)], axis=1)
            term = nt(right, left)
            total = term if total is None else total + term
        prod[g] = total.astype(BF16)
        for r in ring_order(n_g):
            c = d_copy(r)
            c.start()
            sends.append(c)

    def product():
        for r in range(1, n_g):
            d_copy(r).wait_recv()
        return prod[...].reshape(n_g * part_rows, width)

    def z_total(a):
        for r in range(1, n_g):
            z_copy(a, r).wait_recv()
        total = zsend[a, g].astype(F32)
        for r in range(1, n_g):
            total = total + zrecv[a, r - 1].astype(F32)
        return total.astype(BF16)

    def exchange(value, src, dst, ssem, rsem):
        src[...] = value
        copies = []
        for r in ring_order(n_q):
            c = remote(src, dst.at[r - 1], ssem.at[r - 1], rsem.at[r - 1], x_peer(r))
            c.start()
            copies.append(c)
            sends.append(c)
        return copies

    def collected(value, copies, dst):
        for c in copies:
            c.wait_recv()
        half = n_q // 2
        total = None
        for k in range(half):
            first = value.astype(F32) if k == 0 else dst[k - 1].astype(F32)
            pair = first + dst[k + half - 1].astype(F32)
            total = pair if total is None else total + pair
        return total

    def f_exchange(a):
        value = z_total(a)
        return value, exchange(value, fsend.at[a], frecv.at[a], fs_sem.at[a], fr_sem.at[a])

    def fed(a, started):
        value, copies = started
        return rhs_t[a, g] - collected(value, copies, frecv.at[a])

    def y_copy(k, r):
        return remote(ysend.at[k], yrecv.at[k, own_b], ys_sem.at[k, r - 1], yr_sem.at[k, own_b], y_peer(r))

    def broadcast(k, value):
        ysend[k] = value

        @pl.when(own)
        def _():
            for r in ring_order(n_p):
                y_copy(k, r).start()
            yrecv[k, own_b] = value

    def gathered(k):
        for b in range(nb):

            @pl.when(b * n_q + q != p)
            def _(b=b):
                remote(ysend.at[k], yrecv.at[k, b], ys_sem.at[k, 0], yr_sem.at[k, b], y_peer(1)).wait_recv()

        return jnp.concatenate([yrecv[k, b] for b in range(nb)], axis=1)

    def spread_copy(lo, n, r):
        mine = xz.at[g, pl.ds(lo, n)]
        return remote(mine, mine, xs_sem.at[lo, r - 1], xr_sem.at[lo, r - 1], z_peer(r))

    def spread(lo, values):
        for k, value in enumerate(values):
            xz[g, lo + k] = value
        for r in ring_order(n_g):
            c = spread_copy(lo, len(values), r)
            c.start()
            sends.append(c)

    def solve(a, resid):
        return nt(resid.astype(BF16), inv_v[a]).astype(BF16)

    started = f_exchange(0)
    y0 = solve(0, fed(0, started))
    broadcast(0, y0)
    later = [f_exchange(a) for a in (1, 2)]
    fed1, fed2 = [fed(a, later[a - 1]) for a in (1, 2)]

    block0 = gathered(0)
    value = nt(block0, weights(1, 0)).astype(BF16)
    copies = exchange(value, psend.at[0], precv.at[0], ps_sem.at[0], pr_sem.at[0])
    part2 = nt(block0, weights(2, 0))
    y1 = solve(1, fed1 - collected(value, copies, precv.at[0]))
    broadcast(1, y1)
    form_product()
    block1 = gathered(1)
    value = (part2 + nt(block1, weights(2, 1))).astype(BF16)
    copies = exchange(value, psend.at[1], precv.at[1], ps_sem.at[1], pr_sem.at[1])
    part0 = nt(block1, weights(0, 1))
    y2 = solve(2, fed2 - collected(value, copies, precv.at[1]))
    broadcast(2, y2)
    spread(2, [y2])

    weights0 = product()
    block2 = gathered(2)
    part1 = nt(block2, weights(1, 2))
    part0 = part0 + nt(block2, weights(0, 2)) - jnp.dot(block2, weights0, preferred_element_type=F32)
    both = jnp.concatenate([part0, part1], axis=1).astype(BF16)
    copies = exchange(both, bsend, brecv, ps_sem.at[2], pr_sem.at[2])

    def finish(a, full):
        for c in range(n_c):
            span = pl.ds(c * chunk, chunk)
            before = sub_v[span, :].astype(F32) if a == levels - 1 else acc[span, :]
            after = before - nt(up_v[span, a * width : (a + 1) * width], full)
            if a > 0:
                acc[span, :] = after
            else:
                res_v[span, :] = after.astype(BF16)
        x_v[a] = jnp.transpose(full.astype(F32)).astype(BF16)

    total = collected(both, copies, brecv)
    x0 = (y0.astype(F32) - total[:, :width]).astype(BF16)
    x1 = (y1.astype(F32) - total[:, width:]).astype(BF16)
    spread(0, [x0, x1])

    loads[7].wait()
    rows = res_v.shape[0]
    n_c = 4
    chunk = rows // n_c
    for lo, n in ((2, 1), (0, 2)):
        for r in range(1, n_g):
            spread_copy(lo, n, r).wait_recv()
        for a in range(lo + n - 1, lo - 1, -1):
            finish(a, xz[:, a].reshape(n_g * xz.shape[2], width))

    for c in sends:
        c.wait_send()

    @pl.when(own)
    def _():
        for k in range(levels):
            for r in range(1, n_p):
                y_copy(k, r).wait_send()


def store_kernel(x_v, res_v, x_hbm, res_hbm, sem):
    copies = [pltpu.make_async_copy(res_v, res_hbm, sem.at[0]), pltpu.make_async_copy(x_v, x_hbm, sem.at[1])]
    for c in copies:
        c.start()
    for c in copies:
        c.wait()


def per_device(dims, sep_rhs, diag_inverse, off_blocks, pattern, sub_solution, couple_low, couple_up):
    n_g, n_p, n_q, levels, width, n_b = dims
    sub = sub_solution.reshape(sub_solution.shape[-2:])
    low = couple_low.reshape(couple_low.shape[-2:])
    up = couple_up.reshape(couple_up.shape[-2:])
    rhs = sep_rhs.reshape(sep_rhs.shape[1:])
    inv = diag_inverse.reshape(diag_inverse.shape[1:])
    blk = off_blocks.reshape(levels, n_b, width, width)
    rows, cols = sub.shape
    piece = cols // n_g
    nb = n_p // n_q
    dma = pltpu.SemaphoreType.DMA
    wc = nb * width // n_g
    vmem = pltpu.VMEM
    x, res = pl.pallas_call(
        functools.partial(kernel, dims),
        out_shape=(vmem(rhs.shape, BF16), vmem(sub.shape, BF16)),
        in_specs=[pl.BlockSpec(memory_space=pl.ANY)] * 7,
        out_specs=(pl.BlockSpec(memory_space=vmem),) * 2,
        scratch_shapes=[
            vmem(sub.shape, BF16),
            vmem(low.shape, BF16),
            vmem(up.shape, BF16),
            vmem(inv.shape, BF16),
            vmem(rhs.shape, BF16),
            vmem(blk.shape, BF16),
            pltpu.SMEM(pattern.shape, jnp.int32),
            vmem((levels * (levels - 1), width, nb * width), BF16),
            vmem((levels, n_g, piece, width), F32),
            vmem((levels, n_g, piece, width), BF16),
            vmem((levels, n_g - 1, piece, width), BF16),
            vmem((levels, piece, width), BF16),
            vmem((levels, n_q - 1, piece, width), BF16),
            vmem((2, piece, width), BF16),
            vmem((2, n_q - 1, piece, width), BF16),
            vmem((piece, 2 * width), BF16),
            vmem((n_q - 1, piece, 2 * width), BF16),
            vmem((levels, piece, width), BF16),
            vmem((levels, nb, piece, width), BF16),
            vmem((n_g, levels, piece, width), BF16),
            vmem(sub.shape, F32),
            vmem((width // wc, wc, width), BF16),
            vmem((n_p, wc, width), BF16),
            vmem((n_q - 1, width, nb * width), BF16),
            vmem((n_g, wc, width), BF16),
            dma((8,)),
            dma((levels, n_g - 1)),
            dma((levels, n_g - 1)),
            dma((levels, n_q - 1)),
            dma((levels, n_q - 1)),
            dma((levels, n_q - 1)),
            dma((levels, n_q - 1)),
            dma((levels, n_p - 1)),
            dma((levels, nb)),
            dma((levels, n_g - 1)),
            dma((levels, n_g - 1)),
            dma((n_p - 1,)),
            dma((n_p - 1,)),
            dma((n_q - 1,)),
            dma((n_q - 1,)),
            dma((n_g - 1,)),
            dma((n_g - 1,)),
        ],
        compiler_params=pltpu.CompilerParams(collective_id=0, has_side_effects=True),
    )(rhs, inv, blk, pattern, sub, low, up)
    x, res = pl.pallas_call(
        store_kernel,
        out_shape=(jax.ShapeDtypeStruct(rhs.shape, BF16), jax.ShapeDtypeStruct(sub.shape, BF16)),
        in_specs=[pl.BlockSpec(memory_space=vmem)] * 2,
        out_specs=(pl.BlockSpec(memory_space=pl.ANY),) * 2,
        scratch_shapes=[dma((2,))],
    )(*(pltpu.with_memory_space_constraint(v, vmem) for v in (x, res)))
    return x[None], res[None, None, None]


def solution(mesh):
    n_g, n_p, n_q = mesh.shape["gz"], mesh.shape["pr"], mesh.shape["pc"]

    def step(*args):
        levels, width = args[1].shape[1], args[1].shape[2]
        dims = (n_g, n_p, n_q, levels, width, args[2].shape[2])
        return per_device(dims, *args)

    return jax.shard_map(
        step,
        mesh=mesh,
        in_specs=(
            P("pr", None, None, None),
            P("pr", None, None, None),
            P("pr", None, None, "pc", None, None),
            P(),
            P("gz", "pr", "pc", None, None),
            P("gz", "pr", "pc", None, None),
            P("gz", "pr", "pc", None, None),
        ),
        out_specs=(P("pr", None, None, None), P("gz", "pr", "pc", None, None)),
        check_vma=False,
    )
```

time: 64.9 us -> 55.3 us (0.85)
  Pallas kernels: 60.3 us -> 54.3 us
  local copies, waits for them, and re-layouts: 3.21 us -> 0 us
    pallas_call x1 -> x2, Pallas kernels: 60.3 us -> 54.3 us  [the longest x1 53.6 us: per_device(): pl.pallas_call(functools.partial(kernel, dims), out_shape=(vmem(rhs.shape...]
    unnamed x2 -> x0, local copies, waits for them, and re-layouts: 3.21 us -> none
where the time goes in v2:
time: 55.3 us; the launch traced here: 55 us
  Pallas kernels  54.3 us (98%)
  between operations  0.64 us (1%)
    pallas_call x1, Pallas kernels, per_device(): pl.pallas_call(functools.partial(kernel, dims), out_shape=(vmem(rhs.shape...  53.6 us

profile of v2, /device:TPU:1, one launch (start us, length us, event | category | flops | bytes accessed | tf_op | source)
XLA Modules:
  0.0 55.0 jit_solution(6579764575069647356)
XLA Ops:
  0.6 53.6 %shard_map.86 = (bf16[3,128,128]{2,1,0:T(8,128)(2,1)S(1)}, bf16[1024,128]{1,0:T(8,128)(2,1)S(1)}) custom-call(bf16[3,128,128]{2,1,0:T(8,128)(2,1)} %bitcast.12, bf16[3,128,128]{2,1,0:T(8,128)(2,1)} %bitcast.13, bf16[3,12,128,128]{3,2,1,0:T(8,128)(2,1)} %bitcast.8, s32[48,48]{1,0:T(8,128)} %pat_hbm.1, bf16[1024,128]{1,0:T(8,128)(2,1)} %bitcast.11, ...), custom_call_target="tpu_custom_call" | custom-call | tf_op jit(solution)/shard_map/pallas_call | solution.py:341
  54.2 0.7 %shard_map.87 = (bf16[3,128,128]{2,1,0:T(8,128)(2,1)}, bf16[1024,128]{1,0:T(8,128)(2,1)}) custom-call(bf16[3,128,128]{2,1,0:T(8,128)(2,1)S(1)} %get-tuple-element.6.x_v, bf16[1024,128]{1,0:T(8,128)(2,1)S(1)} %get-tuple-element.7.res_v), custom_call_target="tpu_custom_call" | custom-call | tf_op jit(solution)/shard_map/pallas_call | solution.py:392

commit v3 on v2

--- a/solution.py
+++ b/solution.py
@@ -25,8 +25,8 @@
     rhs_hbm, inv_hbm, blk_hbm, pat_hbm, sub_hbm, low_hbm, up_hbm,
     x_v, res_v,
     sub_v, low_v, up_v, inv_v, rhs_v, blk_v, pat_s,
-    w_v, rhs_t, zsend, zrecv, fsend, frecv, psend, precv, bsend, brecv, ysend, yrecv, xz, acc, u_piece, u_all, f_all, prod,
-    in_sem, zs_sem, zr_sem, fs_sem, fr_sem, ps_sem, pr_sem, ys_sem, yr_sem, xs_sem, xr_sem, us_sem, ur_sem, ws_sem, wr_sem, ds_sem, dr_sem,
+    w_v, rhs_t, zsend, zrecv, fsend, frecv, esend, erecv, ysend, yrecv, csend, crecv, l_out, l_in, xz, acc, u_piece, u_all, f_all, prod,
+    in_sem, zs_sem, zr_sem, fs_sem, fr_sem, es_sem, er_sem, cs_sem, cr_sem, ls_sem, lr_sem, vs_sem, vr_sem, ys_sem, yr_sem, xs_sem, xr_sem, us_sem, ur_sem, ws_sem, wr_sem, ds_sem, dr_sem,
 ):
     n_g, n_p, n_q, levels, width, n_b = dims
     g = lax.axis_index("gz")
@@ -46,8 +46,8 @@
         (low_hbm.at[rest], low_v.at[rest]),
         (blk_hbm, blk_v),
         (pat_hbm, pat_s),
+        (inv_hbm, inv_v),
         (rhs_hbm, rhs_v),
-        (inv_hbm, inv_v),
         (up_hbm, up_v),
     )
     loads = [pltpu.make_async_copy(a, b, in_sem.at[k]) for k, (a, b) in enumerate(pairs)]
@@ -62,6 +62,9 @@
 
     def y_peer(r):
         return {"pr": lax.rem(p + r, n_p)}
+
+    def cross_peer(b):
+        return {"pr": b * n_q + q, "pc": lax.rem(p, n_q)}
 
     barrier = pltpu.get_barrier_semaphore()
     for r in ring_order(n_g):
@@ -71,6 +74,11 @@
     for r in ring_order(n_q):
         pl.semaphore_signal(barrier, inc=1, device_id=x_peer(r), device_id_type=MESH)
 
+    @pl.when(jnp.logical_not(own))
+    def _():
+        for b in range(nb):
+            pl.semaphore_signal(barrier, inc=1, device_id=cross_peer(b), device_id_type=MESH)
+
     def remote(src, dst, ssem, rsem, peer):
         return pltpu.make_async_remote_copy(
             src_ref=src, dst_ref=dst, send_sem=ssem, recv_sem=rsem, device_id=peer, device_id_type=MESH
@@ -91,7 +99,7 @@
     loads[0].wait()
     loads[1].wait()
     partial_update(0)
-    pl.semaphore_wait(barrier, n_g + n_p + n_q - 3)
+    pl.semaphore_wait(barrier, n_g + n_p + n_q - 3 + jnp.where(own, 0, nb))
     for r in ring_order(n_g):
         c = z_copy(0, r)
         c.start()
@@ -120,9 +128,34 @@
     def weights(row_level, col_level):
         return w_v[slot_of(row_level, col_level)]
 
+    def fold(level, col_level):
+        slot = slot_of(level, col_level)
+        w_v[slot] = jnp.dot(inv_v[level], w_v[slot], preferred_element_type=F32).astype(BF16)
+
+    for k in (3, 4, 5):
+        loads[k].wait()
+    masked_blocks(2, 1)
+    fold(2, 1)
+    for b in range(nb):
+        l_out[b] = w_v[slot_of(2, 1), :, b * width : (b + 1) * width]
+
+    def l_copy(b):
+        return remote(l_out.at[b], l_in.at[own_b], ls_sem.at[b], lr_sem.at[own_b], cross_peer(b))
+
+    def l_arrival(b):
+        return remote(l_out.at[b], l_in.at[b], ls_sem.at[b], lr_sem.at[b], cross_peer(b))
+
+    for b in range(nb):
+
+        @pl.when(b * n_q + q != p)
+        def _(b=b):
+            l_copy(b).start()
+
+    @pl.when(own)
+    def _():
+        l_in[own_b] = l_out[own_b]
+
     first, second = slot_of(0, 1), slot_of(1, 2)
-    loads[3].wait()
-    loads[4].wait()
     masked_blocks(0, 1)
     masked_blocks(1, 2)
 
@@ -147,14 +180,13 @@
         sends.append(c)
     u_all[p] = u_piece[g % halves]
 
-    loads[5].wait()
+    for row_level in range(1, levels):
+        masked_blocks(row_level, 0)
+        fold(row_level, 0)
+    masked_blocks(0, 2)
+    loads[6].wait()
     for a in range(levels):
         rhs_t[a] = jnp.transpose(rhs_v[a].astype(F32)).reshape(n_g, rhs_t.shape[2], width)
-    for row_level in range(1, levels):
-        for col_level in range(row_level):
-            masked_blocks(row_level, col_level)
-    masked_blocks(0, 2)
-    loads[6].wait()
 
     def form_product():
         for r in range(1, n_p):
@@ -245,75 +277,131 @@
         for k, value in enumerate(values):
             xz[g, lo + k] = value
         for r in ring_order(n_g):
-            c = spread_copy(lo, len(values), r)
+            c = spread_copy(lo, max(len(values), 1), r)
             c.start()
             sends.append(c)
 
     def solve(a, resid):
-        return nt(resid.astype(BF16), inv_v[a]).astype(BF16)
+        return nt(resid.astype(BF16), inv_v[a])
 
     started = f_exchange(0)
-    y0 = solve(0, fed(0, started))
+    y0 = solve(0, fed(0, started)).astype(BF16)
     broadcast(0, y0)
     later = [f_exchange(a) for a in (1, 2)]
-    fed1, fed2 = [fed(a, later[a - 1]) for a in (1, 2)]
+    solved1, solved2 = [solve(a, fed(a, later[a - 1])) for a in (1, 2)]
 
     block0 = gathered(0)
-    value = nt(block0, weights(1, 0)).astype(BF16)
-    copies = exchange(value, psend.at[0], precv.at[0], ps_sem.at[0], pr_sem.at[0])
-    part2 = nt(block0, weights(2, 0))
-    y1 = solve(1, fed1 - collected(value, copies, precv.at[0]))
+    both = jnp.concatenate([nt(block0, weights(a, 0)) for a in (1, 2)], axis=1).astype(BF16)
+    copies = exchange(both, esend.at[0], erecv.at[0], es_sem.at[0], er_sem.at[0])
+    for b in range(nb):
+
+        @pl.when(b * n_q + q != p)
+        def _(b=b):
+            l_arrival(b).wait_recv()
+
+    step2 = l_in[...].reshape(nb * width, width)
+    total = collected(both, copies, erecv.at[0])
+    y1 = (solved1 - total[:, :width]).astype(BF16)
+    terms = nt(y1, step2).astype(BF16)
+    for b in range(nb):
+        csend[b] = terms[:, b * width : (b + 1) * width]
+
+    def c_copy(b):
+        ahead = lax.rem(b * n_q + q + n_p - p, n_p) - 1
+        return remote(csend.at[b], crecv.at[ahead], cs_sem.at[b], cr_sem.at[ahead], {"pr": b * n_q + q})
+
+    for b in range(nb):
+
+        @pl.when(b * n_q + q != p)
+        def _(b=b):
+            c_copy(b).start()
+
     broadcast(1, y1)
     form_product()
     block1 = gathered(1)
-    value = (part2 + nt(block1, weights(2, 1))).astype(BF16)
-    copies = exchange(value, psend.at[1], precv.at[1], ps_sem.at[1], pr_sem.at[1])
     part0 = nt(block1, weights(0, 1))
-    y2 = solve(2, fed2 - collected(value, copies, precv.at[1]))
-    broadcast(2, y2)
-    spread(2, [y2])
+
+    def v_copy(r):
+        mine = xz.at[g, levels - 1]
+        return remote(mine, mine, vs_sem.at[r - 1], vr_sem, x_peer(r))
+
+    @pl.when(own)
+    def _():
+        sum2 = csend[own_b].astype(F32)
+        for r in range(1, n_p):
+            remote(csend.at[0], crecv.at[r - 1], cs_sem.at[0], cr_sem.at[r - 1], y_peer(1)).wait_recv()
+            sum2 = sum2 + crecv[r - 1].astype(F32)
+        y2 = (solved2 - total[:, width:] - sum2).astype(BF16)
+        ysend[2] = y2
+        for r in ring_order(n_p):
+            y_copy(2, r).start()
+        yrecv[2, own_b] = y2
+        xz[g, levels - 1] = y2
+        for r in ring_order(n_q):
+            v_copy(r).start()
 
     weights0 = product()
     block2 = gathered(2)
     part1 = nt(block2, weights(1, 2))
     part0 = part0 + nt(block2, weights(0, 2)) - jnp.dot(block2, weights0, preferred_element_type=F32)
     both = jnp.concatenate([part0, part1], axis=1).astype(BF16)
-    copies = exchange(both, bsend, brecv, ps_sem.at[2], pr_sem.at[2])
-
-    def finish(a, full):
-        for c in range(n_c):
-            span = pl.ds(c * chunk, chunk)
-            before = sub_v[span, :].astype(F32) if a == levels - 1 else acc[span, :]
-            after = before - nt(up_v[span, a * width : (a + 1) * width], full)
-            if a > 0:
-                acc[span, :] = after
-            else:
-                res_v[span, :] = after.astype(BF16)
-        x_v[a] = jnp.transpose(full.astype(F32)).astype(BF16)
-
-    total = collected(both, copies, brecv)
+    copies = exchange(both, esend.at[1], erecv.at[1], es_sem.at[1], er_sem.at[1])
+
+    @pl.when(jnp.logical_not(own))
+    def _():
+        v_copy(1).wait_recv()
+
+    spread(2, [])
+    total = collected(both, copies, erecv.at[1])
     x0 = (y0.astype(F32) - total[:, :width]).astype(BF16)
     x1 = (y1.astype(F32) - total[:, width:]).astype(BF16)
+    early = list(sends)
     spread(0, [x0, x1])
 
     loads[7].wait()
     rows = res_v.shape[0]
     n_c = 4
     chunk = rows // n_c
-    for lo, n in ((2, 1), (0, 2)):
-        for r in range(1, n_g):
-            spread_copy(lo, n, r).wait_recv()
-        for a in range(lo + n - 1, lo - 1, -1):
-            finish(a, xz[:, a].reshape(n_g * xz.shape[2], width))
-
-    for c in sends:
+
+    def full(a):
+        return xz[:, a].reshape(n_g * xz.shape[2], width)
+
+    for r in range(1, n_g):
+        spread_copy(2, 1, r).wait_recv()
+    x2 = full(2)
+    for c in range(n_c):
+        span = pl.ds(c * chunk, chunk)
+        acc[span, :] = sub_v[span, :].astype(F32) - nt(up_v[span, 2 * width :], x2)
+    x_v[2] = jnp.transpose(x2.astype(F32)).astype(BF16)
+
+    for c in early:
         c.wait_send()
+
+    for b in range(nb):
+
+        @pl.when(b * n_q + q != p)
+        def _(b=b):
+            l_copy(b).wait_send()
+            c_copy(b).wait_send()
 
     @pl.when(own)
     def _():
         for k in range(levels):
             for r in range(1, n_p):
                 y_copy(k, r).wait_send()
+        for r in range(1, n_q):
+            v_copy(r).wait_send()
+
+    for r in range(1, n_g):
+        spread_copy(0, 2, r).wait_recv()
+    x01 = jnp.concatenate([full(0), full(1)], axis=1)
+    for c in range(n_c):
+        span = pl.ds(c * chunk, chunk)
+        res_v[span, :] = (acc[span, :] - nt(up_v[span, : 2 * width], x01)).astype(BF16)
+    for a in range(2):
+        x_v[a] = jnp.transpose(full(a).astype(F32)).astype(BF16)
+    for c in sends[len(early) :]:
+        c.wait_send()
 
 
 def store_kernel(x_v, res_v, x_hbm, res_hbm, sem):
@@ -357,12 +445,14 @@
             vmem((levels, n_g - 1, piece, width), BF16),
             vmem((levels, piece, width), BF16),
             vmem((levels, n_q - 1, piece, width), BF16),
-            vmem((2, piece, width), BF16),
-            vmem((2, n_q - 1, piece, width), BF16),
-            vmem((piece, 2 * width), BF16),
-            vmem((n_q - 1, piece, 2 * width), BF16),
+            vmem((2, piece, 2 * width), BF16),
+            vmem((2, n_q - 1, piece, 2 * width), BF16),
             vmem((levels, piece, width), BF16),
             vmem((levels, nb, piece, width), BF16),
+            vmem((nb, piece, width), BF16),
+            vmem((n_p - 1, piece, width), BF16),
+            vmem((nb, width, width), BF16),
+            vmem((nb, width, width), BF16),
             vmem((n_g, levels, piece, width), BF16),
             vmem(sub.shape, F32),
             vmem((width // wc, wc, width), BF16),
@@ -374,8 +464,14 @@
             dma((levels, n_g - 1)),
             dma((levels, n_q - 1)),
             dma((levels, n_q - 1)),
-            dma((levels, n_q - 1)),
-            dma((levels, n_q - 1)),
+            dma((2, n_q - 1)),
+            dma((2, n_q - 1)),
+            dma((nb,)),
+            dma((n_p - 1,)),
+            dma((nb,)),
+            dma((nb,)),
+            dma((n_q - 1,)),
+            dma(()),
             dma((levels, n_p - 1)),
             dma((levels, nb)),
             dma((levels, n_g - 1)),

time: 55.3 us -> 55 us (level)
  Pallas kernels: 54.3 us -> 53.6 us
    pallas_call x1, Pallas kernels: 53.6 us -> 52.9 us  [per_device(): pl.pallas_call(functools.partial(kernel, dims), out_shape=(vmem(rhs.shape...]
where the time goes in v3:
time: 55 us; the launch traced here: 54.3 us
  Pallas kernels  53.6 us (97%)
  between operations  0.64 us (1%)
    pallas_call x1, Pallas kernels, per_device(): pl.pallas_call(functools.partial(kernel, dims), out_shape=(vmem(rhs.shape...  52.9 us

profile of v3, /device:TPU:1, one launch (start us, length us, event | category | flops | bytes accessed | tf_op | source)
XLA Modules:
  0.0 54.3 jit_solution(11824251972907676886)
XLA Ops:
  0.6 52.9 %shard_map.86 = (bf16[3,128,128]{2,1,0:T(8,128)(2,1)S(1)}, bf16[1024,128]{1,0:T(8,128)(2,1)S(1)}) custom-call(bf16[3,128,128]{2,1,0:T(8,128)(2,1)} %bitcast.12, bf16[3,128,128]{2,1,0:T(8,128)(2,1)} %bitcast.13, bf16[3,12,128,128]{3,2,1,0:T(8,128)(2,1)} %bitcast.8, s32[48,48]{1,0:T(8,128)} %pat_hbm.1, bf16[1024,128]{1,0:T(8,128)(2,1)} %bitcast.11, ...), custom_call_target="tpu_custom_call" | custom-call | tf_op jit(solution)/shard_map/pallas_call | solution.py:429
  53.5 0.7 %shard_map.87 = (bf16[3,128,128]{2,1,0:T(8,128)(2,1)}, bf16[1024,128]{1,0:T(8,128)(2,1)}) custom-call(bf16[3,128,128]{2,1,0:T(8,128)(2,1)S(1)} %get-tuple-element.6.x_v, bf16[1024,128]{1,0:T(8,128)(2,1)S(1)} %get-tuple-element.7.res_v), custom_call_target="tpu_custom_call" | custom-call | tf_op jit(solution)/shard_map/pallas_call | solution.py:488

commit v4 on v3

v4 whole, which is shorter than its diff:
```python
import functools

import jax
import jax.numpy as jnp
from jax import lax
from jax.experimental import pallas as pl
from jax.experimental.pallas import tpu as pltpu
from jax.sharding import PartitionSpec as P

F32 = jnp.float32
BF16 = jnp.bfloat16
MESH = pl.DeviceIdType.MESH


def nt(a, b):
    return lax.dot_general(a, b, (((1,), (1,)), ((), ())), preferred_element_type=F32)


def ring_order(n):
    return sorted(range(1, n), key=lambda r: (-min(r, n - r), r))


def kernel(
    dims,
    rhs_hbm, inv_hbm, blk_hbm, pat_hbm, sub_hbm, low_hbm, up_hbm,
    x_out, acc, up01_v,
    sub_v, low_v, up2_v, inv_v, rhs_v, blk_v, pat_s,
    w_v, wl_v, wu_v, rhs_t, zsend, zrecv, fsend, frecv, esend, erecv, ysend, yrecv, csend, crecv, l_out, l_in, xz, u_piece, u_all, f_all, prod,
    in_sem, zs_sem, zr_sem, fs_sem, fr_sem, es_sem, er_sem, cs_sem, cr_sem, ls_sem, lr_sem, vs_sem, vr_sem, ys_sem, yr_sem, xs_sem, xr_sem, us_sem, ur_sem, ws_sem, wr_sem, ds_sem, dr_sem,
):
    n_g, n_p, n_q, levels, width, n_b = dims
    g = lax.axis_index("gz")
    p = lax.axis_index("pr")
    q = lax.axis_index("pc")
    nb = n_p // n_q
    own = lax.rem(p, n_q) == q
    own_b = p // n_q

    part_rows = prod.shape[1]
    halves = width // part_rows

    rest = pl.ds(width, (levels - 1) * width)
    pairs = (
        (sub_hbm, sub_v),
        (low_hbm.at[pl.ds(0, width)], low_v.at[pl.ds(0, width)]),
        (low_hbm.at[rest], low_v.at[rest]),
        (blk_hbm, blk_v),
        (pat_hbm, pat_s),
        (inv_hbm, inv_v),
        (rhs_hbm, rhs_v),
        (up_hbm.at[:, pl.ds(2 * width, width)], up2_v),
        (up_hbm.at[:, pl.ds(0, 2 * width)], up01_v),
    )
    loads = [pltpu.make_async_copy(a, b, in_sem.at[k]) for k, (a, b) in enumerate(pairs)]
    for c in loads:
        c.start()

    def z_peer(r):
        return {"gz": lax.rem(g + r, n_g)}

    def x_peer(r):
        return {"pc": lax.rem(q + r, n_q)}

    def y_peer(r):
        return {"pr": lax.rem(p + r, n_p)}

    def cross_peer(b):
        return {"pr": b * n_q + q, "pc": lax.rem(p, n_q)}

    barrier = pltpu.get_barrier_semaphore()
    for r in ring_order(n_g):
        pl.semaphore_signal(barrier, inc=1, device_id=z_peer(r), device_id_type=MESH)
    for r in ring_order(n_p):
        pl.semaphore_signal(barrier, inc=1, device_id=y_peer(r), device_id_type=MESH)
    for r in ring_order(n_q):
        pl.semaphore_signal(barrier, inc=1, device_id=x_peer(r), device_id_type=MESH)

    @pl.when(jnp.logical_not(own))
    def _():
        for b in range(nb):
            pl.semaphore_signal(barrier, inc=1, device_id=cross_peer(b), device_id_type=MESH)

    def remote(src, dst, ssem, rsem, peer):
        return pltpu.make_async_remote_copy(
            src_ref=src, dst_ref=dst, send_sem=ssem, recv_sem=rsem, device_id=peer, device_id_type=MESH
        )

    drains = []

    def send_all(copies, size, sem):
        for c in copies:
            c.start()
        drains.append((size, sem))

    def sent(size, sem):
        remote(size, size, sem, sem, x_peer(1)).wait_send()

    def arrived(size, sem):
        remote(size, size, sem, sem, x_peer(1)).wait_recv()

    def fewer_if_own(wait, ref, sem):
        @pl.when(own)
        def _():
            wait(ref.at[pl.ds(0, nb - 1)], sem)

        @pl.when(jnp.logical_not(own))
        def _():
            wait(ref, sem)


    def partial_update(a):
        part = jnp.dot(low_v[a * width : (a + 1) * width, :], sub_v[...], preferred_element_type=F32)
        flipped = jnp.transpose(part).astype(BF16)
        zsend[a] = flipped.reshape(n_g, flipped.shape[0] // n_g, width)

    def z_copy(a, r):
        k = min(a, 1)
        return remote(zsend.at[a, lax.rem(g + r, n_g)], zrecv.at[a, r - 1], zs_sem.at[k], zr_sem.at[k], z_peer(r))

    others = pl.ds(1, levels - 1)

    loads[0].wait()
    loads[1].wait()
    partial_update(0)

    def slot_of(row_level, col_level):
        return row_level * (levels - 1) + (col_level if col_level < row_level else col_level - 1)

    def masked_blocks(row_level, col_level):
        for b in range(nb):
            i = row_level * n_p + p
            j = col_level * n_p + b * n_q + q
            mark = pat_s[i, j] if col_level < row_level else pat_s[j, i]
            block = blk_v[row_level, col_level * nb + b]
            w_v[slot_of(row_level, col_level), :, b * width : (b + 1) * width] = jnp.where(
                mark == 1, block, jnp.zeros_like(block)
            )

    def weights(row_level, col_level):
        return w_v[slot_of(row_level, col_level)]

    def folded(level, col_level):
        return jnp.dot(inv_v[level], weights(level, col_level), preferred_element_type=F32).astype(BF16)

    for k in (3, 4, 5):
        loads[k].wait()
    masked_blocks(2, 1)
    step21 = folded(2, 1)
    for b in range(nb):
        l_out[b] = step21[:, b * width : (b + 1) * width]

    def l_copy(b):
        return remote(l_out.at[b], l_in.at[own_b], ls_sem, lr_sem, cross_peer(b))

    @pl.when(own)
    def _():
        l_in[own_b] = l_out[own_b]

    first, second = slot_of(0, 1), slot_of(1, 2)
    masked_blocks(0, 1)
    masked_blocks(1, 2)

    def f_copy(h, r):
        span = pl.ds(h * (nb * width // 2), nb * width // 2)
        return remote(w_v.at[first, :, span], f_all.at[r - 1, :, span], ws_sem, wr_sem, x_peer(r))

    def f_send(h):
        for r in ring_order(n_q):
            f_copy(h, r).start()

    def u_copy(r):
        return remote(u_piece.at[g % halves], u_all.at[p], us_sem, ur_sem, y_peer(r))

    def d_copy(r):
        return remote(prod.at[g], prod.at[g], ds_sem, dr_sem, z_peer(r))

    mine = w_v[second, :, pl.ds(pl.multiple_of(g // halves * width, width), width)]
    u_piece[...] = jnp.transpose(mine.astype(F32)).astype(BF16).reshape(halves, part_rows, width)
    u_all[p] = u_piece[g % halves]

    pl.semaphore_wait(barrier, n_g + n_p + n_q - 3 + jnp.where(own, 0, nb))
    send_all([z_copy(0, r) for r in ring_order(n_g)], zrecv.at[0], zs_sem.at[0])
    f_send(0)
    for b in range(nb):

        @pl.when(b * n_q + q != p)
        def _(b=b):
            l_copy(b).start()

    send_all([u_copy(r) for r in ring_order(n_p)], u_all.at[pl.ds(0, n_p - 1)], us_sem)
    loads[2].wait()
    for a in range(1, levels):
        partial_update(a)
        for r in ring_order(n_g):
            z_copy(a, r).start()
    drains.append((zrecv.at[others], zs_sem.at[1]))

    for row_level in range(1, levels):
        masked_blocks(row_level, 0)
        wl_v[(row_level - 1) * width : row_level * width, :] = folded(row_level, 0)
    masked_blocks(0, 2)
    for k, w in enumerate((weights(0, 2), weights(1, 2))):
        wu_v[:, k * width : (k + 1) * width] = jnp.transpose(w.astype(F32)).astype(BF16)
    loads[6].wait()
    for a in range(levels):
        rhs_t[a] = jnp.transpose(rhs_v[a].astype(F32)).reshape(n_g, rhs_t.shape[2], width)

    def form_product():
        arrived(u_all.at[pl.ds(0, n_p - 1)], ur_sem)
        arrived(f_all, wr_sem)
        total = None
        for r in range(n_q):
            left = weights(0, 1) if r == 0 else f_all[r - 1]
            from_q = lax.rem(q + n_q - r, n_q)
            right = jnp.concatenate([u_all[b * n_q + from_q] for b in range(nb)], axis=1)
            term = nt(right, left)
            total = term if total is None else total + term
        prod[g] = total.astype(BF16)
        send_all([d_copy(r) for r in ring_order(n_g)], prod.at[pl.ds(0, n_g - 1)], ds_sem)

    def product():
        arrived(prod.at[pl.ds(0, n_g - 1)], dr_sem)
        return prod[...].reshape(n_g * part_rows, width)

    def z_total(a):
        total = zsend[a, g].astype(F32)
        for r in range(1, n_g):
            total = total + zrecv[a, r - 1].astype(F32)
        return total.astype(BF16)

    def exchange(value, src, dst, ssem, rsem):
        src[...] = value
        send_all([remote(src, dst.at[r - 1], ssem, rsem, x_peer(r)) for r in ring_order(n_q)], dst, ssem)

    def collected(value, dst, rsem):
        arrived(dst, rsem)
        half = n_q // 2
        total = None
        for k in range(half):
            start = value.astype(F32) if k == 0 else dst[k - 1].astype(F32)
            pair = start + dst[k + half - 1].astype(F32)
            total = pair if total is None else total + pair
        return total

    def y_copy(k, r):
        return remote(ysend.at[k], yrecv.at[k, own_b], ys_sem.at[k], yr_sem.at[k], y_peer(r))

    def broadcast_own(k, value):
        ysend[k] = value
        for r in ring_order(n_p):
            y_copy(k, r).start()
        yrecv[k, own_b] = value

    def gathered(k):
        fewer_if_own(arrived, yrecv.at[k], yr_sem.at[k])
        return jnp.concatenate([yrecv[k, b] for b in range(nb)], axis=1)

    def spread(k, lo, n):
        mine = xz.at[g, pl.ds(lo, n)]
        copies = [remote(mine, mine, xs_sem.at[k], xr_sem.at[k], z_peer(r)) for r in ring_order(n_g)]
        send_all(copies, zrecv.at[pl.ds(lo, n)], xs_sem.at[k])

    def solve(a, resid):
        return nt(resid.astype(BF16), inv_v[a])

    arrived(zrecv.at[0], zr_sem.at[0])
    value = z_total(0)
    exchange(value, fsend, frecv, fs_sem, fr_sem)
    y0 = solve(0, rhs_t[0, g] - collected(value, frecv, fr_sem)).astype(BF16)

    @pl.when(own)
    def _():
        broadcast_own(0, y0)

    arrived(zrecv.at[others], zr_sem.at[1])
    both = jnp.concatenate([z_total(a) for a in (1, 2)], axis=1)
    exchange(both, esend.at[0], erecv.at[0], es_sem.at[0], er_sem.at[0])
    f_send(1)
    drains.append((f_all, ws_sem))
    total = collected(both, erecv.at[0], er_sem.at[0])
    solved1 = solve(1, rhs_t[1, g] - total[:, :width])
    solved2 = solve(2, rhs_t[2, g] - total[:, width:])

    both = nt(gathered(0), wl_v[...]).astype(BF16)
    exchange(both, esend.at[1], erecv.at[1], es_sem.at[1], er_sem.at[1])
    fewer_if_own(arrived, l_in, lr_sem)
    step2 = l_in[...].reshape(nb * width, width)
    total = collected(both, erecv.at[1], er_sem.at[1])
    y1 = (solved1 - total[:, :width]).astype(BF16)
    rest2 = solved2 - total[:, width:]
    terms = nt(y1, step2).astype(BF16)
    for b in range(nb):
        csend[b] = terms[:, b * width : (b + 1) * width]
    for b in range(nb):

        @pl.when(b * n_q + q != p)
        def _(b=b):
            ahead = lax.rem(b * n_q + q + n_p - p, n_p) - 1
            remote(csend.at[b], crecv.at[ahead], cs_sem, cr_sem, {"pr": b * n_q + q}).start()

    @pl.when(own)
    def _():
        broadcast_own(1, y1)

    form_product()

    @pl.when(own)
    def _():
        arrived(crecv, cr_sem)
        sum2 = csend[own_b].astype(F32)
        for r in range(1, n_p):
            sum2 = sum2 + crecv[r - 1].astype(F32)
        y2 = (rest2 - sum2).astype(BF16)
        broadcast_own(2, y2)
        mine = xz.at[g, levels - 1]
        mine[...] = y2
        for r in ring_order(n_q):
            remote(mine, mine, vs_sem, vr_sem, x_peer(r)).start()

    part0 = nt(gathered(1), weights(0, 1))
    weights0 = product()
    wu_v[:, :width] = (wu_v[:, :width].astype(F32) - weights0.astype(F32)).astype(BF16)
    both = jnp.dot(gathered(2), wu_v[...], preferred_element_type=F32)
    both = jnp.concatenate([both[:, :width] + part0, both[:, width:]], axis=1).astype(BF16)
    exchange(both, esend.at[2], erecv.at[2], es_sem.at[2], er_sem.at[2])

    @pl.when(jnp.logical_not(own))
    def _():
        arrived(xz.at[g, levels - 1], vr_sem)

    spread(0, levels - 1, 1)
    total = collected(both, erecv.at[2], er_sem.at[2])
    xz[g, 0] = (y0.astype(F32) - total[:, :width]).astype(BF16)
    xz[g, 1] = (y1.astype(F32) - total[:, width:]).astype(BF16)
    early = list(drains)
    spread(1, 0, 2)

    loads[7].wait()
    rows = acc.shape[0]
    n_c = 4
    chunk = rows // n_c

    def full(a):
        return xz[:, a].reshape(n_g * xz.shape[2], width)

    arrived(zrecv.at[0], xr_sem.at[0])
    x2 = full(2)
    for c in range(n_c):
        span = pl.ds(c * chunk, chunk)
        acc[span, :] = sub_v[span, :].astype(F32) - nt(up2_v[span, :], x2)
    x_out[:, 2 * width :] = x2
    loads[8].wait()
    for size, sem in early:
        sent(size, sem)
    fewer_if_own(sent, l_in, ls_sem)
    fewer_if_own(sent, csend, cs_sem)

    @pl.when(own)
    def _():
        for k in range(levels):
            sent(crecv, ys_sem.at[k])
        sent(frecv, vs_sem)

    arrived(zrecv.at[pl.ds(0, 2)], xr_sem.at[1])
    for a in range(2):
        x_out[:, a * width : (a + 1) * width] = full(a)
    for size, sem in drains[len(early) :]:
        sent(size, sem)


def store_kernel(xt_v, acc, up01_v, x_hbm, res_hbm, x_v, res_v, sem):
    levels, width = x_v.shape[0], x_v.shape[1]
    n_c = 4
    chunk = acc.shape[0] // n_c
    copies = []
    x01 = xt_v[:, : 2 * width]
    for c in range(n_c):
        span = pl.ds(c * chunk, chunk)
        res_v[span, :] = (acc[span, :] - nt(up01_v[span, :], x01)).astype(BF16)
        copies.append(pltpu.make_async_copy(res_v.at[span], res_hbm.at[span], sem.at[c]))
        copies[-1].start()
    for a in range(levels):
        x_v[a] = jnp.transpose(xt_v[:, a * width : (a + 1) * width].astype(F32)).astype(BF16)
    copies.append(pltpu.make_async_copy(x_v, x_hbm, sem.at[n_c]))
    copies[-1].start()
    for c in copies:
        c.wait()


def per_device(dims, sep_rhs, diag_inverse, off_blocks, pattern, sub_solution, couple_low, couple_up):
    n_g, n_p, n_q, levels, width, n_b = dims
    sub = sub_solution.reshape(sub_solution.shape[-2:])
    low = couple_low.reshape(couple_low.shape[-2:])
    up = couple_up.reshape(couple_up.shape[-2:])
    rhs = sep_rhs.reshape(sep_rhs.shape[1:])
    inv = diag_inverse.reshape(diag_inverse.shape[1:])
    blk = off_blocks.reshape(levels, n_b, width, width)
    rows, cols = sub.shape
    piece = cols // n_g
    nb = n_p // n_q
    dma = pltpu.SemaphoreType.DMA
    wc = nb * width // n_g
    vmem = pltpu.VMEM
    xt, acc, up01 = pl.pallas_call(
        functools.partial(kernel, dims),
        out_shape=(vmem((cols, levels * width), BF16), vmem(sub.shape, F32), vmem((rows, 2 * width), BF16)),
        in_specs=[pl.BlockSpec(memory_space=pl.ANY)] * 7,
        out_specs=(pl.BlockSpec(memory_space=vmem),) * 3,
        scratch_shapes=[
            vmem(sub.shape, BF16),
            vmem(low.shape, BF16),
            vmem((rows, width), BF16),
            vmem(inv.shape, BF16),
            vmem(rhs.shape, BF16),
            vmem(blk.shape, BF16),
            pltpu.SMEM(pattern.shape, jnp.int32),
            vmem((levels * (levels - 1), width, nb * width), BF16),
            vmem((2 * width, nb * width), BF16),
            vmem((nb * width, 2 * width), BF16),
            vmem((levels, n_g, piece, width), F32),
            vmem((levels, n_g, piece, width), BF16),
            vmem((levels, n_g - 1, piece, width), BF16),
            vmem((piece, width), BF16),
            vmem((n_q - 1, piece, width), BF16),
            vmem((3, piece, 2 * width), BF16),
            vmem((3, n_q - 1, piece, 2 * width), BF16),
            vmem((levels, piece, width), BF16),
            vmem((levels, nb, piece, width), BF16),
            vmem((nb, piece, width), BF16),
            vmem((n_p - 1, piece, width), BF16),
            vmem((nb, width, width), BF16),
            vmem((nb, width, width), BF16),
            vmem((n_g, levels, piece, width), BF16),
            vmem((width // wc, wc, width), BF16),
            vmem((n_p, wc, width), BF16),
            vmem((n_q - 1, width, nb * width), BF16),
            vmem((n_g, wc, width), BF16),
            dma((9,)),
            dma((2,)),
            dma((2,)),
            dma(()),
            dma(()),
            dma((3,)),
            dma((3,)),
            dma(()),
            dma(()),
            dma(()),
            dma(()),
            dma(()),
            dma(()),
            dma((levels,)),
            dma((levels,)),
            dma((2,)),
            dma((2,)),
            dma(()),
            dma(()),
            dma(()),
            dma(()),
            dma(()),
            dma(()),
        ],
        compiler_params=pltpu.CompilerParams(collective_id=0, has_side_effects=True),
    )(rhs, inv, blk, pattern, sub, low, up)
    x, res = pl.pallas_call(
        store_kernel,
        out_shape=(jax.ShapeDtypeStruct(rhs.shape, BF16), jax.ShapeDtypeStruct(sub.shape, BF16)),
        in_specs=[pl.BlockSpec(memory_space=vmem)] * 3,
        out_specs=(pl.BlockSpec(memory_space=pl.ANY),) * 2,
        scratch_shapes=[vmem(rhs.shape, BF16), vmem(sub.shape, BF16), dma((5,))],
    )(*(pltpu.with_memory_space_constraint(v, vmem) for v in (xt, acc, up01)))
    return x[None], res[None, None, None]


def solution(mesh):
    n_g, n_p, n_q = mesh.shape["gz"], mesh.shape["pr"], mesh.shape["pc"]

    def step(*args):
        levels, width = args[1].shape[1], args[1].shape[2]
        dims = (n_g, n_p, n_q, levels, width, args[2].shape[2])
        return per_device(dims, *args)

    return jax.shard_map(
        step,
        mesh=mesh,
        in_specs=(
            P("pr", None, None, None),
            P("pr", None, None, None),
            P("pr", None, None, "pc", None, None),
            P(),
            P("gz", "pr", "pc", None, None),
            P("gz", "pr", "pc", None, None),
            P("gz", "pr", "pc", None, None),
        ),
        out_specs=(P("pr", None, None, None), P("gz", "pr", "pc", None, None)),
        check_vma=False,
    )
```

time: 55 us -> 50 us (0.909)
  Pallas kernels: 53.6 us -> 48.4 us
    pallas_call x1, Pallas kernels: 52.9 us -> 47.4 us  [per_device(): pl.pallas_call(functools.partial(kernel, dims), out_shape=(vmem((cols, le...]
where the time goes in v4:
time: 50 us; the launch traced here: 49 us
  Pallas kernels  48.4 us (97%)
  between operations  0.64 us (1%)
    pallas_call x1, Pallas kernels, per_device(): pl.pallas_call(functools.partial(kernel, dims), out_shape=(vmem((cols, le...  47.4 us
    pallas_call x1, Pallas kernels, per_device(): pl.pallas_call(store_kernel, out_shape=(jax.ShapeDtypeStruct(rhs.shape, B...  1.03 us

profile of v4, /device:TPU:1, one launch (start us, length us, event | category | flops | bytes accessed | tf_op | source)
XLA Modules:
  0.0 49.0 jit_solution(6294535317823162019)
XLA Ops:
  0.6 47.4 %shard_map.86 = (bf16[128,384]{1,0:T(8,128)(2,1)S(1)}, f32[1024,128]{1,0:T(8,128)S(1)}, bf16[1024,256]{1,0:T(8,128)(2,1)S(1)}) custom-call(bf16[3,128,128]{2,1,0:T(8,128)(2,1)} %bitcast.12, bf16[3,128,128]{2,1,0:T(8,128)(2,1)} %bitcast.13, bf16[3,12,128,128]{3,2,1,0:T(8,128)(2,1)} %bitcast.8, s32[48,48]{1,0:T(8,128)} %pat_hbm.1, bf16[1024,128]{1,0:T(8,128)(2,1)} %bitcast.11, ...), custom_call_target="tpu_custom_call" | custom-call | tf_op jit(solution)/shard_map/pallas_call | solution.py:404
  48.0 1.0 %shard_map.87 = (bf16[3,128,128]{2,1,0:T(8,128)(2,1)}, bf16[1024,128]{1,0:T(8,128)(2,1)}) custom-call(bf16[128,384]{1,0:T(8,128)(2,1)S(1)} %get-tuple-element.7.xt_v, f32[1024,128]{1,0:T(8,128)S(1)} %get-tuple-element.8.acc, bf16[1024,256]{1,0:T(8,128)(2,1)S(1)} %get-tuple-element.9.up01_v), custom_call_target="tpu_custom_call" | custom-call | tf_op jit(solution)/shard_map/pallas_call | solution.py:464

commit v5 on v4

--- a/solution.py
+++ b/solution.py
@@ -25,7 +25,7 @@
     rhs_hbm, inv_hbm, blk_hbm, pat_hbm, sub_hbm, low_hbm, up_hbm,
     x_out, acc, up01_v,
     sub_v, low_v, up2_v, inv_v, rhs_v, blk_v, pat_s,
-    w_v, wl_v, wu_v, rhs_t, zsend, zrecv, fsend, frecv, esend, erecv, ysend, yrecv, csend, crecv, l_out, l_in, xz, u_piece, u_all, f_all, prod,
+    w_v, wl_v, wu_v, inv_t, rhs_t, zsend, zrecv, fsend, frecv, esend, erecv, ysend, yrecv, csend, crecv, l_out, l_in, xz, u_piece, u_all, f_all, prod,
     in_sem, zs_sem, zr_sem, fs_sem, fr_sem, es_sem, er_sem, cs_sem, cr_sem, ls_sem, lr_sem, vs_sem, vr_sem, ys_sem, yr_sem, xs_sem, xr_sem, us_sem, ur_sem, ws_sem, wr_sem, ds_sem, dr_sem,
 ):
     n_g, n_p, n_q, levels, width, n_b = dims
@@ -68,6 +68,11 @@
         return {"pr": b * n_q + q, "pc": lax.rem(p, n_q)}
 
     barrier = pltpu.get_barrier_semaphore()
+    @pl.when(jnp.logical_not(own))
+    def _():
+        for b in range(nb):
+            pl.semaphore_signal(barrier, inc=1, device_id=cross_peer(b), device_id_type=MESH)
+
     for r in ring_order(n_g):
         pl.semaphore_signal(barrier, inc=1, device_id=z_peer(r), device_id_type=MESH)
     for r in ring_order(n_p):
@@ -75,11 +80,6 @@
     for r in ring_order(n_q):
         pl.semaphore_signal(barrier, inc=1, device_id=x_peer(r), device_id_type=MESH)
 
-    @pl.when(jnp.logical_not(own))
-    def _():
-        for b in range(nb):
-            pl.semaphore_signal(barrier, inc=1, device_id=cross_peer(b), device_id_type=MESH)
-
     def remote(src, dst, ssem, rsem, peer):
         return pltpu.make_async_remote_copy(
             src_ref=src, dst_ref=dst, send_sem=ssem, recv_sem=rsem, device_id=peer, device_id_type=MESH
@@ -110,8 +110,8 @@
 
     def partial_update(a):
         part = jnp.dot(low_v[a * width : (a + 1) * width, :], sub_v[...], preferred_element_type=F32)
-        flipped = jnp.transpose(part).astype(BF16)
-        zsend[a] = flipped.reshape(n_g, flipped.shape[0] // n_g, width)
+        turned = jnp.transpose(part).astype(BF16)
+        zsend[a] = turned.reshape(n_g, turned.shape[0] // n_g, width)
 
     def z_copy(a, r):
         k = min(a, 1)
@@ -140,14 +140,17 @@
         return w_v[slot_of(row_level, col_level)]
 
     def folded(level, col_level):
-        return jnp.dot(inv_v[level], weights(level, col_level), preferred_element_type=F32).astype(BF16)
+        return jnp.dot(inv_v[level], weights(level, col_level), preferred_element_type=F32)
+
+    def flipped(a):
+        return jnp.transpose(a.astype(F32)).astype(BF16)
 
     for k in (3, 4, 5):
         loads[k].wait()
     masked_blocks(2, 1)
     step21 = folded(2, 1)
     for b in range(nb):
-        l_out[b] = step21[:, b * width : (b + 1) * width]
+        l_out[b] = flipped(step21[:, b * width : (b + 1) * width])
 
     def l_copy(b):
         return remote(l_out.at[b], l_in.at[own_b], ls_sem, lr_sem, cross_peer(b))
@@ -197,10 +200,11 @@
 
     for row_level in range(1, levels):
         masked_blocks(row_level, 0)
-        wl_v[(row_level - 1) * width : row_level * width, :] = folded(row_level, 0)
+        wl_v[:, (row_level - 1) * width : row_level * width] = flipped(folded(row_level, 0))
     masked_blocks(0, 2)
     for k, w in enumerate((weights(0, 2), weights(1, 2))):
-        wu_v[:, k * width : (k + 1) * width] = jnp.transpose(w.astype(F32)).astype(BF16)
+        wu_v[:, k * width : (k + 1) * width] = flipped(w)
+    inv_t[...] = flipped(inv_v[0])
     loads[6].wait()
     for a in range(levels):
         rhs_t[a] = jnp.transpose(rhs_v[a].astype(F32)).reshape(n_g, rhs_t.shape[2], width)
@@ -255,18 +259,14 @@
         fewer_if_own(arrived, yrecv.at[k], yr_sem.at[k])
         return jnp.concatenate([yrecv[k, b] for b in range(nb)], axis=1)
 
-    def spread(k, lo, n):
-        mine = xz.at[g, pl.ds(lo, n)]
-        copies = [remote(mine, mine, xs_sem.at[k], xr_sem.at[k], z_peer(r)) for r in ring_order(n_g)]
-        send_all(copies, zrecv.at[pl.ds(lo, n)], xs_sem.at[k])
-
     def solve(a, resid):
         return nt(resid.astype(BF16), inv_v[a])
 
     arrived(zrecv.at[0], zr_sem.at[0])
     value = z_total(0)
     exchange(value, fsend, frecv, fs_sem, fr_sem)
-    y0 = solve(0, rhs_t[0, g] - collected(value, frecv, fr_sem)).astype(BF16)
+    resid = (rhs_t[0, g] - collected(value, frecv, fr_sem)).astype(BF16)
+    y0 = jnp.dot(resid, inv_t[...], preferred_element_type=F32).astype(BF16)
 
     @pl.when(own)
     def _():
@@ -281,14 +281,14 @@
     solved1 = solve(1, rhs_t[1, g] - total[:, :width])
     solved2 = solve(2, rhs_t[2, g] - total[:, width:])
 
-    both = nt(gathered(0), wl_v[...]).astype(BF16)
+    both = jnp.dot(gathered(0), wl_v[...], preferred_element_type=F32).astype(BF16)
     exchange(both, esend.at[1], erecv.at[1], es_sem.at[1], er_sem.at[1])
     fewer_if_own(arrived, l_in, lr_sem)
-    step2 = l_in[...].reshape(nb * width, width)
+    step2 = jnp.concatenate([l_in[b] for b in range(nb)], axis=1)
     total = collected(both, erecv.at[1], er_sem.at[1])
     y1 = (solved1 - total[:, :width]).astype(BF16)
     rest2 = solved2 - total[:, width:]
-    terms = nt(y1, step2).astype(BF16)
+    terms = jnp.dot(y1, step2, preferred_element_type=F32).astype(BF16)
     for b in range(nb):
         csend[b] = terms[:, b * width : (b + 1) * width]
     for b in range(nb):
@@ -328,12 +328,21 @@
     def _():
         arrived(xz.at[g, levels - 1], vr_sem)
 
-    spread(0, levels - 1, 1)
+    last = xz.at[g, pl.ds(levels - 1, 1)]
+    copies = [remote(last, last, xs_sem.at[0], xr_sem.at[0], z_peer(r)) for r in ring_order(n_g)]
+    send_all(copies, zrecv.at[pl.ds(0, 1)], xs_sem.at[0])
     total = collected(both, erecv.at[2], er_sem.at[2])
     xz[g, 0] = (y0.astype(F32) - total[:, :width]).astype(BF16)
     xz[g, 1] = (y1.astype(F32) - total[:, width:]).astype(BF16)
     early = list(drains)
-    spread(1, 0, 2)
+    mine = xz.at[g, pl.ds(0, 2)]
+    for plane in range(n_g):
+
+        @pl.when(g != plane)
+        def _(plane=plane):
+            remote(mine, mine, xs_sem.at[1], xr_sem.at[1], {"gz": plane}).start()
+
+    drains.append((zrecv.at[pl.ds(0, 2)], xs_sem.at[1]))
 
     loads[7].wait()
     rows = acc.shape[0]
@@ -348,7 +357,7 @@
     for c in range(n_c):
         span = pl.ds(c * chunk, chunk)
         acc[span, :] = sub_v[span, :].astype(F32) - nt(up2_v[span, :], x2)
-    x_out[:, 2 * width :] = x2
+    x_out[:, 2 * width :] = flipped(x2)
     loads[8].wait()
     for size, sem in early:
         sent(size, sem)
@@ -369,20 +378,21 @@
 
 
 def store_kernel(xt_v, acc, up01_v, x_hbm, res_hbm, x_v, res_v, sem):
-    levels, width = x_v.shape[0], x_v.shape[1]
+    width = x_v.shape[1]
     n_c = 4
     chunk = acc.shape[0] // n_c
-    copies = []
-    x01 = xt_v[:, : 2 * width]
+    for a in range(2):
+        x_v[a] = jnp.transpose(xt_v[:, a * width : (a + 1) * width].astype(F32)).astype(BF16)
+    x_v[2] = xt_v[:, 2 * width :]
+    copies = [pltpu.make_async_copy(x_v, x_hbm, sem.at[n_c])]
+    x01 = x_v[0:2].reshape(2 * width, width)
     for c in range(n_c):
         span = pl.ds(c * chunk, chunk)
-        res_v[span, :] = (acc[span, :] - nt(up01_v[span, :], x01)).astype(BF16)
+        term = jnp.dot(up01_v[span, :], x01, preferred_element_type=F32)
+        res_v[span, :] = (acc[span, :] - term).astype(BF16)
         copies.append(pltpu.make_async_copy(res_v.at[span], res_hbm.at[span], sem.at[c]))
         copies[-1].start()
-    for a in range(levels):
-        x_v[a] = jnp.transpose(xt_v[:, a * width : (a + 1) * width].astype(F32)).astype(BF16)
-    copies.append(pltpu.make_async_copy(x_v, x_hbm, sem.at[n_c]))
-    copies[-1].start()
+    copies[0].start()
     for c in copies:
         c.wait()
 
@@ -415,8 +425,9 @@
             vmem(blk.shape, BF16),
             pltpu.SMEM(pattern.shape, jnp.int32),
             vmem((levels * (levels - 1), width, nb * width), BF16),
-            vmem((2 * width, nb * width), BF16),
             vmem((nb * width, 2 * width), BF16),
+            vmem((nb * width, 2 * width), BF16),
+            vmem((width, width), BF16),
             vmem((levels, n_g, piece, width), F32),
             vmem((levels, n_g, piece, width), BF16),
             vmem((levels, n_g - 1, piece, width), BF16),

time: 50 us -> 49.6 us (level)
  no operation moved by 1% of the time
where the time goes in v5:
time: 49.6 us; the launch traced here: 48.8 us
  Pallas kernels  48.1 us (97%)
  between operations  0.64 us (1%)
    pallas_call x1, Pallas kernels, per_device(): pl.pallas_call(functools.partial(kernel, dims), out_shape=(vmem((cols, le...  47 us
    pallas_call x1, Pallas kernels, per_device(): pl.pallas_call(store_kernel, out_shape=(jax.ShapeDtypeStruct(rhs.shape, B...  1.13 us

profile of v5, /device:TPU:1, one launch (start us, length us, event | category | flops | bytes accessed | tf_op | source)
XLA Modules:
  0.0 48.8 jit_solution(3373838334156702087)
XLA Ops:
  0.6 47.0 %shard_map.86 = (bf16[128,384]{1,0:T(8,128)(2,1)S(1)}, f32[1024,128]{1,0:T(8,128)S(1)}, bf16[1024,256]{1,0:T(8,128)(2,1)S(1)}) custom-call(bf16[3,128,128]{2,1,0:T(8,128)(2,1)} %bitcast.12, bf16[3,128,128]{2,1,0:T(8,128)(2,1)} %bitcast.13, bf16[3,12,128,128]{3,2,1,0:T(8,128)(2,1)} %bitcast.8, s32[48,48]{1,0:T(8,128)} %pat_hbm.1, bf16[1024,128]{1,0:T(8,128)(2,1)} %bitcast.11, ...), custom_call_target="tpu_custom_call" | custom-call | tf_op jit(solution)/shard_map/pallas_call | solution.py:414
  47.7 1.1 %shard_map.87 = (bf16[3,128,128]{2,1,0:T(8,128)(2,1)}, bf16[1024,128]{1,0:T(8,128)(2,1)}) custom-call(bf16[128,384]{1,0:T(8,128)(2,1)S(1)} %get-tuple-element.7.xt_v, f32[1024,128]{1,0:T(8,128)S(1)} %get-tuple-element.8.acc, bf16[1024,256]{1,0:T(8,128)(2,1)S(1)} %get-tuple-element.9.up01_v), custom_call_target="tpu_custom_call" | custom-call | tf_op jit(solution)/shard_map/pallas_call | solution.py:475

commit v6 on v5

--- a/solution.py
+++ b/solution.py
@@ -39,6 +39,31 @@
     part_rows = prod.shape[1]
     halves = width // part_rows
 
+    def z_peer(r):
+        return {"gz": lax.rem(g + r, n_g)}
+
+    def x_peer(r):
+        return {"pc": lax.rem(q + r, n_q)}
+
+    def y_peer(r):
+        return {"pr": lax.rem(p + r, n_p)}
+
+    def cross_peer(b):
+        return {"pr": b * n_q + q, "pc": lax.rem(p, n_q)}
+
+    barrier = pltpu.get_barrier_semaphore()
+    @pl.when(jnp.logical_not(own))
+    def _():
+        for b in range(nb):
+            pl.semaphore_signal(barrier, inc=1, device_id=cross_peer(b), device_id_type=MESH)
+
+    for r in ring_order(n_g):
+        pl.semaphore_signal(barrier, inc=1, device_id=z_peer(r), device_id_type=MESH)
+    for r in ring_order(n_p):
+        pl.semaphore_signal(barrier, inc=1, device_id=y_peer(r), device_id_type=MESH)
+    for r in ring_order(n_q):
+        pl.semaphore_signal(barrier, inc=1, device_id=x_peer(r), device_id_type=MESH)
+
     rest = pl.ds(width, (levels - 1) * width)
     pairs = (
         (sub_hbm, sub_v),
@@ -55,31 +80,6 @@
     for c in loads:
         c.start()
 
-    def z_peer(r):
-        return {"gz": lax.rem(g + r, n_g)}
-
-    def x_peer(r):
-        return {"pc": lax.rem(q + r, n_q)}
-
-    def y_peer(r):
-        return {"pr": lax.rem(p + r, n_p)}
-
-    def cross_peer(b):
-        return {"pr": b * n_q + q, "pc": lax.rem(p, n_q)}
-
-    barrier = pltpu.get_barrier_semaphore()
-    @pl.when(jnp.logical_not(own))
-    def _():
-        for b in range(nb):
-            pl.semaphore_signal(barrier, inc=1, device_id=cross_peer(b), device_id_type=MESH)
-
-    for r in ring_order(n_g):
-        pl.semaphore_signal(barrier, inc=1, device_id=z_peer(r), device_id_type=MESH)
-    for r in ring_order(n_p):
-        pl.semaphore_signal(barrier, inc=1, device_id=y_peer(r), device_id_type=MESH)
-    for r in ring_order(n_q):
-        pl.semaphore_signal(barrier, inc=1, device_id=x_peer(r), device_id_type=MESH)
-
     def remote(src, dst, ssem, rsem, peer):
         return pltpu.make_async_remote_copy(
             src_ref=src, dst_ref=dst, send_sem=ssem, recv_sem=rsem, device_id=peer, device_id_type=MESH
@@ -115,7 +115,7 @@
 
     def z_copy(a, r):
         k = min(a, 1)
-        return remote(zsend.at[a, lax.rem(g + r, n_g)], zrecv.at[a, r - 1], zs_sem.at[k], zr_sem.at[k], z_peer(r))
+        return remote(zsend.at[a, lax.rem(g + r, n_g)], zrecv.at[a, r - 1], zs_sem, zr_sem.at[k], z_peer(r))
 
     others = pl.ds(1, levels - 1)
 
@@ -181,8 +181,12 @@
     u_piece[...] = jnp.transpose(mine.astype(F32)).astype(BF16).reshape(halves, part_rows, width)
     u_all[p] = u_piece[g % halves]
 
+    loads[2].wait()
+    for a in range(1, levels):
+        partial_update(a)
     pl.semaphore_wait(barrier, n_g + n_p + n_q - 3 + jnp.where(own, 0, nb))
-    send_all([z_copy(0, r) for r in ring_order(n_g)], zrecv.at[0], zs_sem.at[0])
+    for r in ring_order(n_g):
+        z_copy(0, r).start()
     f_send(0)
     for b in range(nb):
 
@@ -191,12 +195,10 @@
             l_copy(b).start()
 
     send_all([u_copy(r) for r in ring_order(n_p)], u_all.at[pl.ds(0, n_p - 1)], us_sem)
-    loads[2].wait()
     for a in range(1, levels):
-        partial_update(a)
         for r in ring_order(n_g):
             z_copy(a, r).start()
-    drains.append((zrecv.at[others], zs_sem.at[1]))
+    drains.append((zrecv, zs_sem))
 
     for row_level in range(1, levels):
         masked_blocks(row_level, 0)
@@ -234,7 +236,8 @@
 
     def exchange(value, src, dst, ssem, rsem):
         src[...] = value
-        send_all([remote(src, dst.at[r - 1], ssem, rsem, x_peer(r)) for r in ring_order(n_q)], dst, ssem)
+        for r in ring_order(n_q):
+            remote(src, dst.at[r - 1], ssem, rsem, x_peer(r)).start()
 
     def collected(value, dst, rsem):
         arrived(dst, rsem)
@@ -274,15 +277,15 @@
 
     arrived(zrecv.at[others], zr_sem.at[1])
     both = jnp.concatenate([z_total(a) for a in (1, 2)], axis=1)
-    exchange(both, esend.at[0], erecv.at[0], es_sem.at[0], er_sem.at[0])
-    f_send(1)
-    drains.append((f_all, ws_sem))
+    exchange(both, esend.at[0], erecv.at[0], es_sem, er_sem.at[0])
     total = collected(both, erecv.at[0], er_sem.at[0])
     solved1 = solve(1, rhs_t[1, g] - total[:, :width])
     solved2 = solve(2, rhs_t[2, g] - total[:, width:])
 
     both = jnp.dot(gathered(0), wl_v[...], preferred_element_type=F32).astype(BF16)
-    exchange(both, esend.at[1], erecv.at[1], es_sem.at[1], er_sem.at[1])
+    exchange(both, esend.at[1], erecv.at[1], es_sem, er_sem.at[1])
+    f_send(1)
+    drains.append((f_all, ws_sem))
     fewer_if_own(arrived, l_in, lr_sem)
     step2 = jnp.concatenate([l_in[b] for b in range(nb)], axis=1)
     total = collected(both, erecv.at[1], er_sem.at[1])
@@ -317,20 +320,24 @@
         for r in ring_order(n_q):
             remote(mine, mine, vs_sem, vr_sem, x_peer(r)).start()
 
+    drains.append((frecv, fs_sem))
+    drains.append((erecv, es_sem))
+
     part0 = nt(gathered(1), weights(0, 1))
     weights0 = product()
     wu_v[:, :width] = (wu_v[:, :width].astype(F32) - weights0.astype(F32)).astype(BF16)
     both = jnp.dot(gathered(2), wu_v[...], preferred_element_type=F32)
     both = jnp.concatenate([both[:, :width] + part0, both[:, width:]], axis=1).astype(BF16)
-    exchange(both, esend.at[2], erecv.at[2], es_sem.at[2], er_sem.at[2])
+    exchange(both, esend.at[2], erecv.at[2], es_sem, er_sem.at[2])
 
     @pl.when(jnp.logical_not(own))
     def _():
         arrived(xz.at[g, levels - 1], vr_sem)
 
     last = xz.at[g, pl.ds(levels - 1, 1)]
-    copies = [remote(last, last, xs_sem.at[0], xr_sem.at[0], z_peer(r)) for r in ring_order(n_g)]
-    send_all(copies, zrecv.at[pl.ds(0, 1)], xs_sem.at[0])
+    copies = [remote(last, last, xs_sem, xr_sem.at[0], z_peer(r)) for r in ring_order(n_g)]
+    for c in copies:
+        c.start()
     total = collected(both, erecv.at[2], er_sem.at[2])
     xz[g, 0] = (y0.astype(F32) - total[:, :width]).astype(BF16)
     xz[g, 1] = (y1.astype(F32) - total[:, width:]).astype(BF16)
@@ -340,9 +347,9 @@
 
         @pl.when(g != plane)
         def _(plane=plane):
-            remote(mine, mine, xs_sem.at[1], xr_sem.at[1], {"gz": plane}).start()
-
-    drains.append((zrecv.at[pl.ds(0, 2)], xs_sem.at[1]))
+            remote(mine, mine, xs_sem, xr_sem.at[1], {"gz": plane}).start()
+
+    drains.append((zrecv, xs_sem))
 
     loads[7].wait()
     rows = acc.shape[0]
@@ -447,11 +454,11 @@
             vmem((n_q - 1, width, nb * width), BF16),
             vmem((n_g, wc, width), BF16),
             dma((9,)),
+            dma(()),
             dma((2,)),
-            dma((2,)),
-            dma(()),
-            dma(()),
-            dma((3,)),
+            dma(()),
+            dma(()),
+            dma(()),
             dma((3,)),
             dma(()),
             dma(()),
@@ -461,7 +468,7 @@
             dma(()),
             dma((levels,)),
             dma((levels,)),
-            dma((2,)),
+            dma(()),
             dma((2,)),
             dma(()),
             dma(()),

time: 49.6 us -> 49.5 us (level)
  no operation moved by 1% of the time
where the time goes in v6:
time: 49.5 us; the launch traced here: 48.7 us
  Pallas kernels  48 us (97%)
  between operations  0.64 us (1%)
    pallas_call x1, Pallas kernels, per_device(): pl.pallas_call(functools.partial(kernel, dims), out_shape=(vmem((cols, le...  46.9 us
    pallas_call x1, Pallas kernels, per_device(): pl.pallas_call(store_kernel, out_shape=(jax.ShapeDtypeStruct(rhs.shape, B...  1.13 us

profile of v6, /device:TPU:1, one launch (start us, length us, event | category | flops | bytes accessed | tf_op | source)
XLA Modules:
  0.0 48.7 jit_solution(17581052175967100829)
XLA Ops:
  0.6 46.9 %shard_map.86 = (bf16[128,384]{1,0:T(8,128)(2,1)S(1)}, f32[1024,128]{1,0:T(8,128)S(1)}, bf16[1024,256]{1,0:T(8,128)(2,1)S(1)}) custom-call(bf16[3,128,128]{2,1,0:T(8,128)(2,1)} %bitcast.12, bf16[3,128,128]{2,1,0:T(8,128)(2,1)} %bitcast.13, bf16[3,12,128,128]{3,2,1,0:T(8,128)(2,1)} %bitcast.8, s32[48,48]{1,0:T(8,128)} %pat_hbm.1, bf16[1024,128]{1,0:T(8,128)(2,1)} %bitcast.11, ...), custom_call_target="tpu_custom_call" | custom-call | tf_op jit(solution)/shard_map/pallas_call | solution.py:421
  47.5 1.1 %shard_map.87 = (bf16[3,128,128]{2,1,0:T(8,128)(2,1)}, bf16[1024,128]{1,0:T(8,128)(2,1)}) custom-call(bf16[128,384]{1,0:T(8,128)(2,1)S(1)} %get-tuple-element.7.xt_v, f32[1024,128]{1,0:T(8,128)S(1)} %get-tuple-element.8.acc, bf16[1024,256]{1,0:T(8,128)(2,1)S(1)} %get-tuple-element.9.up01_v), custom_call_target="tpu_custom_call" | custom-call | tf_op jit(solution)/shard_map/pallas_call | solution.py:482
